TPU v7x, 256 devices: a whole 4x4x8 slice. The times are simulated.
256 devices in a mesh: dp: 2 (over core), blk: 128 (over z, x, y).
Axes of the slice: x: 4, y: 4, z: 8, core: 2. Of those that a mesh axis runs over, the one named last changes fastest.
Arguments:
- features: bfloat16 [2, 65536, 128], P('dp', 'blk'), may hold values from -24 to 24
- tile_mask: int32 [2, 128], P('dp', 'blk'), may hold values 0 or 1
- w_first: bfloat16 [3456, 128], replicated, may hold values from -0.109375 to 0.109375
- w_second: bfloat16 [3456, 128], replicated, may hold values from -0.109375 to 0.109375
- cotangent: bfloat16 [2, 65536, 128], P('dp', 'blk'), may hold values from -6 to 6
Outputs:
- grad_first: float32 [3456, 128], replicated
- grad_second: float32 [3456, 128], replicated
- feature_grad: bfloat16 [2, 65536, 128], P('dp', 'blk')
All inputs are finite; a program needn't handle non-finite values. No bound on the sum of `tile_mask` on one device may be relied on, other than what follows from the above.
Results may differ from a plain program's by a relative error of at most 0.0039.
Values may be sent and summed in bfloat16 or wider, within the bound.
A program may use at most 64 MiB of HBM per device.

v0:
```python
import jax
import jax.numpy as jnp
from jax import lax
from jax.sharding import PartitionSpec as P

TILE = 8


unscale = 1.0 / 512.0


def shifted(value, axis, steps):
    count = lax.axis_size(axis)
    leading, last = (max(0, -steps), min(count, count - steps))
    return lax.ppermute(value, axis, [(source, source + steps) for source in range(leading, last)])


def stack_depth(padded, depth_z):
    return jnp.concatenate(
        [padded[:, :, shift_z : shift_z + depth_z, :] for shift_z in range(3)], axis=-1
    )


def arrange(weight):
    width_in = weight.shape[0] // 27
    width_out = weight.shape[1]
    shaped = weight.reshape(width_in, 3, 3, 3, width_out).transpose(1, 2, 3, 0, 4)
    return shaped.reshape(3, 3, 3 * width_in, width_out)


def arrange_flipped(weight):
    width_in = weight.shape[0] // 27
    width_out = weight.shape[1]
    shaped = weight.reshape(width_in, 3, 3, 3, width_out)[:, ::-1, ::-1, ::-1, :].transpose(
        1, 2, 3, 4, 0
    )
    return shaped.reshape(3, 3, 3 * width_out, width_in)


def convolve(padded, kernel):
    size_x = padded.shape[0] - 2
    size_y = padded.shape[1] - 2
    size_z = padded.shape[2] - 2
    stacked = stack_depth(padded, size_z)
    summed = jnp.zeros((size_x * size_y * size_z, kernel.shape[-1]), jnp.float32)
    for step_x in range(3):
        for step_y in range(3):
            slab_rows = stacked[step_x : step_x + size_x, step_y : step_y + size_y].reshape(
                -1, stacked.shape[-1]
            )
            summed = summed + jnp.dot(
                slab_rows, kernel[step_x, step_y], preferred_element_type=jnp.float32
            )
    return summed


def correlate(padded, grads):
    size_x = padded.shape[0] - 2
    size_y = padded.shape[1] - 2
    size_z = padded.shape[2] - 2
    width_in = padded.shape[3]
    width_out = grads.shape[1]
    stacked = stack_depth(padded, size_z)
    blocks = []
    for step_x in range(3):
        for step_y in range(3):
            slab_rows = stacked[step_x : step_x + size_x, step_y : step_y + size_y].reshape(
                -1, stacked.shape[-1]
            )
            blocks.append(
                lax.dot_general(
                    slab_rows, grads, (((0,), (0,)), ((), ())), preferred_element_type=jnp.float32
                )
            )
    joined = jnp.stack(blocks).reshape(3, 3, 3, width_in, width_out).transpose(3, 0, 1, 2, 4)
    return joined.reshape(27 * width_in, width_out)


def direct_rims(values, place, extent):
    padded = jnp.pad(values, ((1, 1), (1, 1), (1, 1), (0, 0)))
    for shift_x in (-1, 0, 1):
        for shift_y in (-1, 0, 1):
            for shift_z in (-1, 0, 1):
                moves = (shift_x, shift_y, shift_z)
                if moves == (0, 0, 0):
                    continue
                sliced = values
                inside = jnp.asarray(True)
                starts = []
                for axis_pos in range(3):
                    toward = moves[axis_pos]
                    length = values.shape[axis_pos]
                    if toward == 1:
                        sliced = lax.slice_in_dim(sliced, 0, 1, axis=axis_pos)
                        starts.append(length + 1)
                    elif toward == -1:
                        sliced = lax.slice_in_dim(sliced, length - 1, length, axis=axis_pos)
                        starts.append(0)
                    else:
                        starts.append(1)
                    inside = (
                        inside
                        & (place[axis_pos] + toward >= 0)
                        & (place[axis_pos] + toward < extent[axis_pos])
                    )
                offset = shift_x * 16 + shift_y * 4 + shift_z
                arrived = shifted(sliced, "blk", -offset)
                arrived = jnp.where(inside, arrived, jnp.zeros_like(arrived))
                padded = lax.dynamic_update_slice(
                    padded, arrived, (starts[0], starts[1], starts[2], 0)
                )
    return padded


def surround(values, place, extent):
    return direct_rims(values, place, extent)


def reduce_rows(term):
    return lax.psum(term, ("dp", "blk"))


def on_device(features, tile_mask, w_first, w_second, cotangent):
    width = features.shape[2]
    size_x = tile_mask.shape[1] * TILE
    region = (size_x, TILE, TILE, width)
    device_index = lax.axis_index("blk")
    place = (device_index // 16, device_index // 4 % 4, device_index % 4)
    extent = (lax.axis_size("blk") // 16, 4, 4)
    keep_rows = jnp.repeat(tile_mask[0], TILE * TILE * TILE).astype(jnp.bfloat16)[:, None]
    keep_float = keep_rows.astype(jnp.float32)
    inputs = features[0] * keep_rows
    grads_out = cotangent[0] * keep_rows
    pad_in = surround(inputs.reshape(region), place, extent)
    pre_act = convolve(pad_in, arrange(w_first))
    hidden = (jax.nn.silu(pre_act) * keep_float).astype(jnp.bfloat16)
    pad_hidden = surround(hidden.reshape(region), place, extent)
    pad_grads = surround(grads_out.reshape(region), place, extent)
    grad_second = reduce_rows(correlate(pad_hidden, grads_out) * unscale)
    back = convolve(pad_grads, arrange_flipped(w_second))
    sigma = jax.nn.sigmoid(pre_act)
    pre_grad = (back * sigma * (1.0 + pre_act * (1.0 - sigma)) * keep_float).astype(jnp.bfloat16)
    pad_pre = surround(pre_grad.reshape(region), place, extent)
    grad_first = reduce_rows(correlate(pad_in, pre_grad) * unscale)
    summed = grads_out.astype(jnp.float32) + convolve(pad_pre, arrange_flipped(w_first))
    result = (summed * keep_float).astype(jnp.bfloat16)
    return (grad_first, grad_second, result[None])


def solution(mesh):
    in_specs = (P("dp", "blk", None), P("dp", "blk"), P(), P(), P("dp", "blk", None))
    out_specs = (P(), P(), P("dp", "blk", None))
    return jax.shard_map(
        on_device, mesh=mesh, in_specs=in_specs, out_specs=out_specs, check_vma=False
    )
```

profile of v0, /device:TPU:1, one launch (start us, length us, event | category | flops | bytes accessed | tf_op | source)
XLA Modules:
  0.0 1219.7 jit_solution(1918076127340199430)
XLA Ops:
  13.9 7.6 collective-permute-start.8
  61.8 5.7 collective-permute-start.32
  68.2 7.6 collective-permute-start.2
  88.1 7.0 collective-permute-start.26
  103.5 6.6 collective-permute-done.51
  111.9 13.2 %collective-permute-done.23 = bf16[1,1,1,128]{3,2,1,0:T(2,128)(2,1)S(1)} collective-permute-done((bf16[1,1,1,128]{3,2,1,0:T(2,128)(2,1)S(1)}, bf16[1,1,1,128]{3,2,1,0:T(2,128)(2,1)S(1)}, u32[]{:S(2)}, u32[]{:S(2)}) %collective-permute-start.23) | collective-permute-done | bytes 288 | tf_op jit(solution)/shard_map/ppermute | solution.py:15
  126.5 11.6 collective-permute-done.49
  145.8 7.1 collective-permute-done.45
  154.8 10.1 collective-permute-done.17
  166.2 6.6 collective-permute-done.43
  184.6 6.0 collective-permute-done.40
  211.9 7.4 collective-permute-start.9
  220.1 11.8 collective-permute-start.5
  232.6 6.9 collective-permute-start.31
  240.3 6.0 collective-permute-start.3
  247.0 13.4 %collective-permute-start.29 = (bf16[1,8,1,128]{3,2,1,0:T(2,128)(2,1)S(1)}, bf16[1,8,1,128]{3,2,1,0:T(2,128)(2,1)S(1)}, u32[]{:S(2)}, u32[]{:S(2)}) collective-permute-start(bf16[1,8,1,128]{3,2,1,0:T(2,128)(2,1)S(1)} %copy-done.21), channel_id=1, source_target_pairs={{0,17},{1,18},{2,19},{3,20},{4,21},{5,22},{6,23},{7,24},{8,25},{9,... | collective-permute-start | bytes 6152 | tf_op jit(solution)/shard_map/ppermute | solution.py:15
  262.4 8.6 collective-permute-done.22
  278.5 11.8 collective-permute-done.20
  291.6 8.1 collective-permute-done.46
  307.2 14.8 %collective-permute-start.1 = (bf16[1,1,8,128]{3,2,1,0:T(8,128)(2,1)S(1)}, bf16[1,1,8,128]{3,2,1,0:T(8,128)(2,1)S(1)}, u32[]{:S(2)}, u32[]{:S(2)}) collective-permute-start(bf16[1,1,8,128]{3,2,1,0:T(8,128)(2,1)S(1)} %copy-done.40), channel_id=1, source_target_pairs={{0,20},{1,21},{2,22},{3,23},{4,24},{5,25},{6,26},{7,27},{8,28},{9,... | collective-permute-start | bytes 6152 | tf_op jit(solution)/shard_map/ppermute | solution.py:15
  340.8 10.8 collective-permute-done.18
  374.8 6.9 collective-permute-start.36
  437.2 17.0 %collective-permute-start.82 = (bf16[1,8,8,128]{3,2,1,0:T(8,128)(2,1)S(1)}, bf16[1,8,8,128]{3,2,1,0:T(8,128)(2,1)}, u32[]{:S(2)}, u32[]{:S(2)}) collective-permute-start(bf16[1,8,8,128]{3,2,1,0:T(8,128)(2,1)S(1)} %get-tuple-element.54), channel_id=1, source_target_pairs={{0,16},{1,17},{2,18},{3,19},{4,20},{5,21},{6,22},{7,23},{8,24},{9,... | collective-permute-start | bytes 49160 | tf_op jit(solution)/shard_map/ppermute | solution.py:15
  459.1 7.6 collective-permute-start.56
  479.7 12.3 %collective-permute-start.80 = (bf16[1,1,1,128]{3,2,1,0:T(2,128)(2,1)}, bf16[1,1,1,128]{3,2,1,0:T(2,128)(2,1)S(1)}, u32[]{:S(2)}, u32[]{:S(2)}) collective-permute-start(bf16[1,1,1,128]{3,2,1,0:T(2,128)(2,1)} %get-tuple-element.103), channel_id=1, source_target_pairs={{0,19},{1,20},{2,21},{3,22},{4,23},{5,24},{6,25},{7,26},{8,27},{9,... | collective-permute-start | bytes 776 | tf_op jit(solution)/shard_map/ppermute | solution.py:15
  492.8 8.6 collective-permute-start.78
  509.7 7.5 collective-permute-done.101
  518.5 6.8 collective-permute-done.97
  526.7 8.4 collective-permute-done.95
  540.9 6.6 collective-permute-start.58
  568.7 10.3 collective-permute-done.75
  580.3 7.7 collective-permute-done.71
  589.3 8.5 collective-permute-done.69
  611.8 6.4 collective-permute-start.61
  626.0 8.9 collective-permute-done.92
  639.9 5.8 collective-permute-start.87
  646.7 7.8 collective-permute-start.83
  655.2 7.8 collective-permute-start.81
  670.9 15.2 %collective-permute-done.98 = bf16[1,8,1,128]{3,2,1,0:T(2,128)(2,1)S(1)} collective-permute-done((bf16[1,8,1,128]{3,2,1,0:T(2,128)(2,1)}, bf16[1,8,1,128]{3,2,1,0:T(2,128)(2,1)S(1)}, u32[]{:S(2)}, u32[]{:S(2)}) %collective-permute-start.98) | collective-permute-done | bytes 2080 | tf_op jit(solution)/shard_map/ppermute | solution.py:15
  686.1 6.0 collective-permute-start.57
  693.1 9.9 collective-permute-start.55
  711.2 12.0 collective-permute-done.72
  725.4 8.4 collective-permute-start.79
  741.8 8.0 collective-permute-done.96
  754.9 5.8 collective-permute-start.53
  768.6 7.7 collective-permute-done.70
  795.2 5.8 collective-permute-start.88
  826.5 382.2 %all-reduce.7.cloned.1.call-done = (f32[3456,128]{1,0:T(8,128)}, f32[3456,128]{1,0:T(8,128)}) async-done(((f32[3456,128]{1,0:T(8,128)}, f32[3456,128]{1,0:T(8,128)}), (f32[3456,128]{1,0:T(8,128)}, f32[3456,128]{1,0:T(8,128)})) %all-reduce.7.cloned.1.call-update) | async-done | bytes 3538960 | tf_op jit(solution)/shard_map/psum | solution.py:120
  (610 shorter events, 407.0 us)
Async XLA Ops:
  7.2 1201.6 %all-reduce.7.cloned.1.call-start = ((), (), s32[]{:S(2)}) async-start(), calls=%async_computation | async-start | bytes 7077888 | tf_op jit(solution)/shard_map/psum | solution.py:120
  8.9 365.8 %collective-permute-start.4 = (bf16[1,8,8,128]{3,2,1,0:T(8,128)(2,1)S(1)}, bf16[1,8,8,128]{3,2,1,0:T(8,128)(2,1)S(1)}, u32[]{:S(2)}, u32[]{:S(2)}) collective-permute-start(bf16[1,8,8,128]{3,2,1,0:T(8,128)(2,1)S(1)} %get-tuple-element.84), channel_id=1, source_target_pairs={{0,16},{1,17},{2,18},{3,19},{4,20},{5,21},{6,22},{7,23},{8,24},{9,... | collective-permute-start | bytes 49160 | tf_op jit(solution)/shard_map/ppermute | solution.py:15
  13.9 38.1 %collective-permute-start.8 = (bf16[1,1,1,128]{3,2,1,0:T(2,128)(2,1)}, bf16[1,1,1,128]{3,2,1,0:T(2,128)(2,1)}, u32[]{:S(2)}, u32[]{:S(2)}) collective-permute-start(bf16[1,1,1,128]{3,2,1,0:T(2,128)(2,1)} %get-tuple-element.149), channel_id=1, source_target_pairs={{0,11},{1,12},{2,13},{3,14},{4,15},{5,16},{6,17},{7,18},{8,19},{9,... | collective-permute-start | bytes 776 | tf_op jit(solution)/shard_map/ppermute | solution.py:15
  21.5 361.6 %collective-permute-start.21 = (bf16[1,8,8,128]{3,2,1,0:T(8,128)(2,1)S(1)}, bf16[1,8,8,128]{3,2,1,0:T(8,128)(2,1)S(1)}, u32[]{:S(2)}, u32[]{:S(2)}) collective-permute-start(bf16[1,8,8,128]{3,2,1,0:T(8,128)(2,1)S(1)} %get-tuple-element.83), channel_id=1, source_target_pairs={{16,0},{17,1},{18,2},{19,3},{20,4},{21,5},{22,6},{23,7},{24,8},{25... | collective-permute-start | bytes 49160 | tf_op jit(solution)/shard_map/ppermute | solution.py:15
  22.8 396.5 %collective-permute-start.47 = (bf16[1,8,8,128]{3,2,1,0:T(8,128)(2,1)S(1)}, bf16[1,8,8,128]{3,2,1,0:T(8,128)(2,1)S(1)}, u32[]{:S(2)}, u32[]{:S(2)}) collective-permute-start(bf16[1,8,8,128]{3,2,1,0:T(8,128)(2,1)S(1)} %get-tuple-element.73), channel_id=1, source_target_pairs={{16,0},{17,1},{18,2},{19,3},{20,4},{21,5},{22,6},{23,7},{24,8},{25... | collective-permute-start | bytes 49160 | tf_op jit(solution)/shard_map/ppermute | solution.py:15
  24.1 372.0 %collective-permute-start.30 = (bf16[1,8,8,128]{3,2,1,0:T(8,128)(2,1)S(1)}, bf16[1,8,8,128]{3,2,1,0:T(8,128)(2,1)}, u32[]{:S(2)}, u32[]{:S(2)}) collective-permute-start(bf16[1,8,8,128]{3,2,1,0:T(8,128)(2,1)S(1)} %get-tuple-element.74), channel_id=1, source_target_pairs={{0,16},{1,17},{2,18},{3,19},{4,20},{5,21},{6,22},{7,23},{8,24},{9,... | collective-permute-start | bytes 49160 | tf_op jit(solution)/shard_map/ppermute | solution.py:15
  68.2 8.4 collective-permute-start.2
  88.1 7.7 collective-permute-start.26
  102.1 7.9 collective-permute-start.51
  110.1 15.1 %collective-permute-start.23 = (bf16[1,1,1,128]{3,2,1,0:T(2,128)(2,1)S(1)}, bf16[1,1,1,128]{3,2,1,0:T(2,128)(2,1)S(1)}, u32[]{:S(2)}, u32[]{:S(2)}) collective-permute-start(bf16[1,1,1,128]{3,2,1,0:T(2,128)(2,1)S(1)} %copy-done.51), channel_id=1, source_target_pairs={{19,0},{20,1},{21,2},{22,3},{23,4},{24,5},{25,6},{26,7},{27,8},{28... | collective-permute-start | bytes 776 | tf_op jit(solution)/shard_map/ppermute | solution.py:15
  125.2 12.9 %collective-permute-start.49 = (bf16[1,1,1,128]{3,2,1,0:T(2,128)(2,1)S(1)}, bf16[1,1,1,128]{3,2,1,0:T(2,128)(2,1)S(1)}, u32[]{:S(2)}, u32[]{:S(2)}) collective-permute-start(bf16[1,1,1,128]{3,2,1,0:T(2,128)(2,1)S(1)} %copy-done.52), channel_id=1, source_target_pairs={{19,0},{20,1},{21,2},{22,3},{23,4},{24,5},{25,6},{26,7},{27,8},{28... | collective-permute-start | bytes 776 | tf_op jit(solution)/shard_map/ppermute | solution.py:15
  144.5 8.4 collective-permute-start.45
  152.9 12.0 collective-permute-start.17
  164.9 7.9 collective-permute-start.43
  211.9 8.2 collective-permute-start.9
  220.1 12.5 %collective-permute-start.5 = (bf16[1,8,1,128]{3,2,1,0:T(2,128)(2,1)S(1)}, bf16[1,8,1,128]{3,2,1,0:T(2,128)(2,1)S(1)}, u32[]{:S(2)}, u32[]{:S(2)}) collective-permute-start(bf16[1,8,1,128]{3,2,1,0:T(2,128)(2,1)S(1)} %copy-done.23), channel_id=1, source_target_pairs={{0,15},{1,16},{2,17},{3,18},{4,19},{5,20},{6,21},{7,22},{8,23},{9,... | collective-permute-start | bytes 6152 | tf_op jit(solution)/shard_map/ppermute | solution.py:15
  247.0 14.2 %collective-permute-start.29 = (bf16[1,8,1,128]{3,2,1,0:T(2,128)(2,1)S(1)}, bf16[1,8,1,128]{3,2,1,0:T(2,128)(2,1)S(1)}, u32[]{:S(2)}, u32[]{:S(2)}) collective-permute-start(bf16[1,8,1,128]{3,2,1,0:T(2,128)(2,1)S(1)} %copy-done.21), channel_id=1, source_target_pairs={{0,17},{1,18},{2,19},{3,20},{4,21},{5,22},{6,23},{7,24},{8,25},{9,... | collective-permute-start | bytes 6152 | tf_op jit(solution)/shard_map/ppermute | solution.py:15
  261.1 10.0 collective-permute-start.22
  276.6 13.7 %collective-permute-start.20 = (bf16[1,8,1,128]{3,2,1,0:T(2,128)(2,1)S(1)}, bf16[1,8,1,128]{3,2,1,0:T(2,128)(2,1)S(1)}, u32[]{:S(2)}, u32[]{:S(2)}) collective-permute-start(bf16[1,8,1,128]{3,2,1,0:T(2,128)(2,1)S(1)} %get-tuple-element.148), channel_id=1, source_target_pairs={{15,0},{16,1},{17,2},{18,3},{19,4},{20,5},{21,6},{22,7},{23,8},{24... | collective-permute-start | bytes 6152 | tf_op jit(solution)/shard_map/ppermute | solution.py:15
  290.3 9.4 collective-permute-start.46
  307.2 15.5 %collective-permute-start.1 = (bf16[1,1,8,128]{3,2,1,0:T(8,128)(2,1)S(1)}, bf16[1,1,8,128]{3,2,1,0:T(8,128)(2,1)S(1)}, u32[]{:S(2)}, u32[]{:S(2)}) collective-permute-start(bf16[1,1,8,128]{3,2,1,0:T(8,128)(2,1)S(1)} %copy-done.40), channel_id=1, source_target_pairs={{0,20},{1,21},{2,22},{3,23},{4,24},{5,25},{6,26},{7,27},{8,28},{9,... | collective-permute-start | bytes 6152 | tf_op jit(solution)/shard_map/ppermute | solution.py:15
  338.9 12.7 %collective-permute-start.18 = (bf16[1,1,8,128]{3,2,1,0:T(8,128)(2,1)S(1)}, bf16[1,1,8,128]{3,2,1,0:T(8,128)(2,1)S(1)}, u32[]{:S(2)}, u32[]{:S(2)}) collective-permute-start(bf16[1,1,8,128]{3,2,1,0:T(8,128)(2,1)S(1)} %copy-done.36), channel_id=1, source_target_pairs={{12,0},{13,1},{14,2},{15,3},{16,4},{17,5},{18,6},{19,7},{20,8},{21... | collective-permute-start | bytes 6152 | tf_op jit(solution)/shard_map/ppermute | solution.py:15
  373.4 21.9 %collective-permute-start.41 = (bf16[8,1,8,128]{3,2,1,0:T(8,128)(2,1)}, bf16[8,1,8,128]{3,2,1,0:T(8,128)(2,1)}, u32[]{:S(2)}, u32[]{:S(2)}) collective-permute-start(bf16[8,1,8,128]{3,2,1,0:T(8,128)(2,1)} %get-tuple-element.79), channel_id=1, source_target_pairs={{4,0},{5,1},{6,2},{7,3},{8,4},{9,5},{10,6},{11,7},{12,8},{13,9},{1... | collective-permute-start | bytes 49160 | tf_op jit(solution)/shard_map/ppermute | solution.py:15
  374.8 21.3 %collective-permute-start.36 = (bf16[8,1,8,128]{3,2,1,0:T(8,128)(2,1)}, bf16[8,1,8,128]{3,2,1,0:T(8,128)(2,1)}, u32[]{:S(2)}, u32[]{:S(2)}) collective-permute-start(bf16[8,1,8,128]{3,2,1,0:T(8,128)(2,1)} %get-tuple-element.80), channel_id=1, source_target_pairs={{0,4},{1,5},{2,6},{3,7},{4,8},{5,9},{6,10},{7,11},{8,12},{9,13},{1... | collective-permute-start | bytes 49160 | tf_op jit(solution)/shard_map/ppermute | solution.py:15
  436.0 375.8 %collective-permute-start.99 = (bf16[1,8,8,128]{3,2,1,0:T(8,128)(2,1)S(1)}, bf16[1,8,8,128]{3,2,1,0:T(8,128)(2,1)S(1)}, u32[]{:S(2)}, u32[]{:S(2)}) collective-permute-start(bf16[1,8,8,128]{3,2,1,0:T(8,128)(2,1)S(1)} %get-tuple-element.53), channel_id=1, source_target_pairs={{16,0},{17,1},{18,2},{19,3},{20,4},{21,5},{22,6},{23,7},{24,8},{25... | collective-permute-start | bytes 49160 | tf_op jit(solution)/shard_map/ppermute | solution.py:15
  437.2 373.0 %collective-permute-start.82 = (bf16[1,8,8,128]{3,2,1,0:T(8,128)(2,1)S(1)}, bf16[1,8,8,128]{3,2,1,0:T(8,128)(2,1)}, u32[]{:S(2)}, u32[]{:S(2)}) collective-permute-start(bf16[1,8,8,128]{3,2,1,0:T(8,128)(2,1)S(1)} %get-tuple-element.54), channel_id=1, source_target_pairs={{0,16},{1,17},{2,18},{3,19},{4,20},{5,21},{6,22},{7,23},{8,24},{9,... | collective-permute-start | bytes 49160 | tf_op jit(solution)/shard_map/ppermute | solution.py:15
  457.8 344.8 %collective-permute-start.73 = (bf16[1,8,8,128]{3,2,1,0:T(8,128)(2,1)S(1)}, bf16[1,8,8,128]{3,2,1,0:T(8,128)(2,1)}, u32[]{:S(2)}, u32[]{:S(2)}) collective-permute-start(bf16[1,8,8,128]{3,2,1,0:T(8,128)(2,1)S(1)} %get-tuple-element.63), channel_id=1, source_target_pairs={{16,0},{17,1},{18,2},{19,3},{20,4},{21,5},{22,6},{23,7},{24,8},{25... | collective-permute-start | bytes 49160 | tf_op jit(solution)/shard_map/ppermute | solution.py:15
  459.1 336.0 %collective-permute-start.56 = (bf16[1,8,8,128]{3,2,1,0:T(8,128)(2,1)S(1)}, bf16[1,8,8,128]{3,2,1,0:T(8,128)(2,1)}, u32[]{:S(2)}, u32[]{:S(2)}) collective-permute-start(bf16[1,8,8,128]{3,2,1,0:T(8,128)(2,1)S(1)} %get-tuple-element.64), channel_id=1, source_target_pairs={{0,16},{1,17},{2,18},{3,19},{4,20},{5,21},{6,22},{7,23},{8,24},{9,... | collective-permute-start | bytes 49160 | tf_op jit(solution)/shard_map/ppermute | solution.py:15
  468.6 8.1 collective-permute-start.86
  479.7 13.0 %collective-permute-start.80 = (bf16[1,1,1,128]{3,2,1,0:T(2,128)(2,1)}, bf16[1,1,1,128]{3,2,1,0:T(2,128)(2,1)S(1)}, u32[]{:S(2)}, u32[]{:S(2)}) collective-permute-start(bf16[1,1,1,128]{3,2,1,0:T(2,128)(2,1)} %get-tuple-element.103), channel_id=1, source_target_pairs={{0,19},{1,20},{2,21},{3,22},{4,23},{5,24},{6,25},{7,26},{8,27},{9,... | collective-permute-start | bytes 776 | tf_op jit(solution)/shard_map/ppermute | solution.py:15
  492.8 9.3 collective-permute-start.78
  508.4 8.8 collective-permute-start.101
  517.2 8.1 collective-permute-start.97
  525.4 9.7 collective-permute-start.95
  567.4 11.6 collective-permute-start.75
  579.0 9.0 collective-permute-start.71
  588.0 9.9 collective-permute-start.69
  624.7 10.2 collective-permute-start.92
  646.7 8.5 collective-permute-start.83
  655.2 8.7 collective-permute-start.81
  669.6 16.5 %collective-permute-start.98 = (bf16[1,8,1,128]{3,2,1,0:T(2,128)(2,1)}, bf16[1,8,1,128]{3,2,1,0:T(2,128)(2,1)S(1)}, u32[]{:S(2)}, u32[]{:S(2)}) collective-permute-start(bf16[1,8,1,128]{3,2,1,0:T(2,128)(2,1)} %get-tuple-element.100), channel_id=1, source_target_pairs={{15,0},{16,1},{17,2},{18,3},{19,4},{20,5},{21,6},{22,7},{23,8},{24... | collective-permute-start | bytes 6152 | tf_op jit(solution)/shard_map/ppermute | solution.py:15
  693.1 10.9 collective-permute-start.55
  709.8 13.3 %collective-permute-start.72 = (bf16[1,8,1,128]{3,2,1,0:T(2,128)(2,1)}, bf16[1,8,1,128]{3,2,1,0:T(2,128)(2,1)S(1)}, u32[]{:S(2)}, u32[]{:S(2)}) collective-permute-start(bf16[1,8,1,128]{3,2,1,0:T(2,128)(2,1)} %get-tuple-element.116), channel_id=1, source_target_pairs={{15,0},{16,1},{17,2},{18,3},{19,4},{20,5},{21,6},{22,7},{23,8},{24... | collective-permute-start | bytes 6152 | tf_op jit(solution)/shard_map/ppermute | solution.py:15
  725.4 9.4 collective-permute-start.79
  740.5 9.3 collective-permute-start.96
  767.3 9.0 collective-permute-start.70
  793.9 16.4 %collective-permute-start.93 = (bf16[8,1,8,128]{3,2,1,0:T(8,128)(2,1)}, bf16[8,1,8,128]{3,2,1,0:T(8,128)(2,1)S(1)}, u32[]{:S(2)}, u32[]{:S(2)}) collective-permute-start(bf16[8,1,8,128]{3,2,1,0:T(8,128)(2,1)} %get-tuple-element.59), channel_id=1, source_target_pairs={{4,0},{5,1},{6,2},{7,3},{8,4},{9,5},{10,6},{11,7},{12,8},{13,9},{1... | collective-permute-start | bytes 49160 | tf_op jit(solution)/shard_map/ppermute | solution.py:15
  795.2 15.1 %collective-permute-start.88 = (bf16[8,1,8,128]{3,2,1,0:T(8,128)(2,1)}, bf16[8,1,8,128]{3,2,1,0:T(8,128)(2,1)S(1)}, u32[]{:S(2)}, u32[]{:S(2)}) collective-permute-start(bf16[8,1,8,128]{3,2,1,0:T(8,128)(2,1)} %get-tuple-element.60), channel_id=1, source_target_pairs={{0,4},{1,5},{2,6},{3,7},{4,8},{5,9},{6,10},{7,11},{8,12},{9,13},{1... | collective-permute-start | bytes 49160 | tf_op jit(solution)/shard_map/ppermute | solution.py:15
  (118 other events, 7093.0 us)
Sparse Core Ops, SparseCore 0:
  822.5 386.1 all-reduce.6
where the time goes:
time: 1230 us; the launch traced here: 1220 us
  waiting for transfers between devices  708 us (58%)
  starting transfers between devices  377 us (31%)
  local copies, waits for them, and re-layouts  88.6 us (7%)
  between operations  17.8 us (1%)
  matrix products  15.2 us (1%)
  other arithmetic  13.3 us (1%)
    psum x1, waiting for transfers between devices, reduce_rows(): return lax.psum(term, ('dp', 'blk'))  382 us
    ppermute x104, starting transfers between devices, shifted(): lax.ppermute(value, axis, [(source, source + steps) for source in range(l...  377 us
    ppermute x104, waiting for transfers between devices, shifted(): lax.ppermute(value, axis, [(source, source + steps) for source in range(l...  325 us
    dynamic_update_slice x104, local copies, waits for them, and re-layouts, direct_rims(): lax.dynamic_update_slice(padded, arrived, (starts[0], starts[1], starts[2...  36 us
  transfers between devices with their start and end apart: 105, of which 90 were waited for; matrix products, arithmetic and copies ran while one was open for 7% of the time, Pallas kernels for 0%

commit v1 on v0

v1 whole, which is shorter than its diff:
```python
import functools

import jax
import jax.numpy as jnp
from jax import lax
from jax.experimental import pallas as pl
from jax.experimental.pallas import tpu as pltpu
from jax.sharding import PartitionSpec as P

T = 8
C = 128
TAPS = 27
K3 = 9 * C
UNSCALE = 1.0 / 512.0
ZS = 24
MESH = pl.DeviceIdType.MESH

DIRS = [
    (i, j, k)
    for i in (-1, 0, 1)
    for j in (-1, 0, 1)
    for k in (-1, 0, 1)
    if (i, j, k) != (0, 0, 0)
]
DIRS.sort(key=lambda d: -sum(abs(v) for v in d))
SIZES = [T if sum(abs(v) for v in d) == 1 else 1 for d in DIRS]
OFFS = [sum(SIZES[:n]) for n in range(len(DIRS))]
TILES = sum(SIZES)
INDEX = {d: n for n, d in enumerate(DIRS)}


def opposite(d):
    return (-d[0], -d[1], -d[2])


def boundary_tiles(d, halo):
    def at(v):
        if halo:
            return 0 if v < 0 else T + 1
        return 1 if v < 0 else T

    dx, dy, dz = d
    xs = range(1, T + 1) if dx == 0 else [at(dx)]
    ys = range(1, T + 1) if dy == 0 else [at(dy)]
    row = lambda x, y, z: (x * (T + 2) + y) * ZS + z + 7
    if dz == 0:
        return [(row(x, y, 1), 1, T) for x in xs for y in ys]
    z = at(dz)
    if dy == 0:
        return [(row(x, 1, z), ZS, T) for x in xs]
    if dx == 0:
        return [(row(1, ys[0], z), (T + 2) * ZS, T)]
    return [(row(xs[0], ys[0], z), 1, 1)]


def rows_of(start, stride, size):
    return pl.ds(start, size) if stride == 1 else pl.ds(start, size, stride=stride)


class Plan:
    def __init__(self, nz, nx, ny):
        self.nz, self.nx, self.ny = nz, nx, ny
        self.n1 = nx
        self.r1 = 64 // nx
        self.t2 = -(-TAPS // ny)
        self.t3 = -(-self.t2 // nz)
        self.slots = self.t3 * nz


def kernel(
    plan,
    mask_ref, feat_hbm, cot_hbm, w1_hbm, w2_hbm,
    fg_ref, g1_ref, g2_ref,
    feat, cot, w1, w2, wf, w1r, w2r, b1,
    pad_i, pad_g, pad_p, st_i, st_g, st_p,
    send_a, recv_a, send_b, recv_b,
    in_t, hid_t, pg_own,
    grads, r0, s1_send, s1_recv, s1_buf, s2_send, s2_recv, s2_buf, s3_recv, ag,
    load_sem, ha_send, ha_recv, hb_send, hb_recv, red_send, red_recv,
):
    nz, nx, ny = plan.nz, plan.nx, plan.ny
    n1, n2, r1, t2, t3 = nx, ny, plan.r1, plan.t2, plan.t3
    core = lax.axis_index("dp")
    blk = lax.axis_index("blk")
    cz = blk // (nx * ny)
    cx = (blk // ny) % nx
    cy = blk % ny

    loads = [
        pltpu.make_async_copy(src, dst, load_sem.at[n])
        for n, (src, dst) in enumerate(((feat_hbm, feat), (cot_hbm, cot), (w1_hbm, w1), (w2_hbm, w2)))
    ]
    for copy in loads:
        copy.start()

    recv_a[...] = jnp.zeros_like(recv_a)
    recv_b[...] = jnp.zeros_like(recv_b)

    step1 = ny - (ny - 1) * core
    step2 = 1 + (ny - 1) * core
    c1 = cx + (cy - cx) * core
    c2 = cy + (cx - cy) * core
    base1 = blk - c1 * step1
    base2 = blk - c2 * step2
    plane = blk - cz * (nx * ny)

    def peer1(k):
        return (core, base1 + (c1 + k) % n1 * step1)

    def peer2(k):
        return (core, base2 + (c2 + k) % n2 * step2)

    def peerz(k):
        return (core, plane + (cz + k) % nz * (nx * ny))

    partner = (1 - core, blk)

    def valid(d):
        inside = None
        for place, count, v in ((cz, nz, d[0]), (cx, nx, d[1]), (cy, ny, d[2])):
            if v == 0:
                continue
            test = place < count - 1 if v > 0 else place > 0
            inside = test if inside is None else jnp.logical_and(inside, test)
        return inside

    def neighbour(d):
        return (core, blk + d[0] * (nx * ny) + d[1] * ny + d[2])

    barrier = pltpu.get_barrier_semaphore()
    count = jnp.int32(1 + (n1 - 1) + (n2 - 1) + (nz - 1))
    peers = [partner] + [peer1(k) for k in range(1, n1)] + [peer2(k) for k in range(1, n2)]
    peers += [peerz(k) for k in range(1, nz)]
    for peer in peers:
        pl.semaphore_signal(barrier, inc=1, device_id=peer, device_id_type=MESH)
    for d in DIRS:
        if sum(abs(v) for v in d) > 1:
            here = valid(d)
            count = count + here.astype(jnp.int32)

            @pl.when(here)
            def _():
                pl.semaphore_signal(barrier, inc=1, device_id=neighbour(d), device_id_type=MESH)

    keep = mask_ref[0, 0].astype(jnp.float32)

    def fill_own(pad, values):
        pad3 = pad.reshape((T + 2) * (T + 2), ZS, C)
        for x in range(T):
            pad3[(x + 1) * (T + 2) + 1:(x + 1) * (T + 2) + 1 + T, 8:16, :] = (
                values[x * 64:(x + 1) * 64].reshape(T, T, C)
            )

    def stage(d, pad, send, base):
        for n, (start, stride, size) in enumerate(boundary_tiles(d, False)):
            send[base + n, 0:size] = pad[rows_of(start, stride, size), :].astype(jnp.bfloat16)

    def fill_halo(d, pad, recv, base):
        for n, (start, stride, size) in enumerate(boundary_tiles(d, True)):
            pad[rows_of(start, stride, size), :] = recv[base + n, 0:size].astype(jnp.float32)

    def halo_copy(d, send, recv, send_sem, recv_sem, arrays):
        there = opposite(d)
        size = SIZES[INDEX[d]] * arrays
        return pltpu.make_async_remote_copy(
            src_ref=send.at[pl.ds(OFFS[INDEX[d]] * arrays, size)],
            dst_ref=recv.at[pl.ds(OFFS[INDEX[there]] * arrays, size)],
            send_sem=send_sem.at[INDEX[d]],
            recv_sem=recv_sem.at[INDEX[there]],
            device_id=neighbour(d),
            device_id_type=MESH,
        )

    def halo_start(*args):
        for d in DIRS:
            @pl.when(valid(d))
            def _():
                halo_copy(d, *args).start()

    def halo_wait(*args):
        for d in DIRS:
            @pl.when(valid(d))
            def _():
                halo_copy(opposite(d), *args).wait_recv()

    def halo_sent(*args):
        for d in DIRS:
            @pl.when(valid(d))
            def _():
                halo_copy(d, *args).wait_send()

    def build(pad, stacked, reverse):
        pad3 = pad.reshape((T + 2) * (T + 2), ZS, C)

        def body(x, carry):
            for c in range(3):
                shift_z = 2 - c if reverse else c
                column = pad3[pl.ds(x * (T + 2), T + 2), 7 + shift_z:15 + shift_z, :]
                for b in range(3):
                    shift_y = 2 - b if reverse else b
                    lanes = (3 * b + c) * C
                    stacked[x, :, lanes:lanes + C] = (
                        column[shift_y:shift_y + T].reshape(64, C).astype(jnp.bfloat16)
                    )
            return carry

        lax.fori_loop(0, T + 2, body, 0)

    def slab(stacked, a):
        return stacked[a:a + T].reshape(512, K3)

    loads[0].wait()
    loads[1].wait()
    inputs = feat[...].astype(jnp.float32) * keep
    grads_out = cot[...].astype(jnp.float32) * keep
    fill_own(pad_i, inputs)
    fill_own(pad_g, grads_out)
    for d in DIRS:
        size = SIZES[INDEX[d]]
        stage(d, pad_i, send_a, OFFS[INDEX[d]] * 2)
        stage(d, pad_g, send_a, OFFS[INDEX[d]] * 2 + size)
    pl.semaphore_wait(barrier, count)
    args_a = (send_a, recv_a, ha_send, ha_recv, 2)
    halo_start(*args_a)

    in_t[...] = inputs.T.astype(jnp.bfloat16)
    loads[2].wait()
    loads[3].wait()
    for w, arranged, stacked in ((w1, w1r, b1), (w2, w2r, None)):
        wf[...] = w[...].astype(jnp.float32)

        def arrange(n, carry):
            row = pl.multiple_of(n * 16, 16)
            for tap in range(TAPS):
                part = wf[pl.ds(n * (16 * TAPS) + tap, 16, stride=TAPS), :].astype(jnp.bfloat16)
                arranged[pl.ds(row, 16), tap * C:(tap + 1) * C] = part
                if stacked is not None:
                    stacked[pl.ds(pl.multiple_of(tap * C + n * 16, 16), 16), :] = part
            return carry

        lax.fori_loop(0, C // 16, arrange, 0)

    halo_wait(*args_a)
    for d in DIRS:
        size = SIZES[INDEX[d]]
        fill_halo(d, pad_i, recv_a, OFFS[INDEX[d]] * 2)
        fill_halo(d, pad_g, recv_a, OFFS[INDEX[d]] * 2 + size)
    build(pad_i, st_i, False)
    build(pad_g, st_g, True)

    def conv_back(stacked, weight):
        total = None
        for a in range(3):
            term = lax.dot_general(
                slab(stacked, 2 - a), weight[:, a * K3:(a + 1) * K3],
                (((1,), (1,)), ((), ())), preferred_element_type=jnp.float32,
            )
            total = term if total is None else total + term
        return total

    def corr(lhs_t, stacked, out):
        for a in range(3):
            out[:, a * K3:(a + 1) * K3] = jnp.dot(
                lhs_t[...], slab(stacked, 2 - a), preferred_element_type=jnp.float32
            )

    pre_act = None
    for a in range(3):
        term = jnp.dot(slab(st_i, a), b1[a * K3:(a + 1) * K3, :], preferred_element_type=jnp.float32)
        pre_act = term if pre_act is None else pre_act + term
    back = conv_back(st_g, w2r)
    sigma = 1.0 / (1.0 + jnp.exp(-pre_act))
    hid_t[...] = (pre_act * sigma * keep).T.astype(jnp.bfloat16)
    pre_grad = back * sigma * (1.0 + pre_act * (1.0 - sigma)) * keep
    fill_own(pad_p, pre_grad)
    for d in DIRS:
        stage(d, pad_p, send_b, OFFS[INDEX[d]])
    args_b = (send_b, recv_b, hb_send, hb_recv, 1)
    halo_start(*args_b)

    def remote(src, dst, g, n, peer):
        return pltpu.make_async_remote_copy(
            src_ref=src, dst_ref=dst, send_sem=red_send.at[g, n], recv_sem=red_recv.at[g, n],
            device_id=peer, device_id_type=MESH,
        )

    S0, S1 = 0, 1
    S2 = S1 + n1 - 1
    S3 = S2 + n2 - 1
    A3 = S3 + nz - 1
    A2 = A3 + nz - 1
    A1 = A2 + n2 - 1
    A0 = A1 + n1 - 1
    mine = pl.multiple_of(core * 64, 64)
    other = pl.multiple_of(64 - core * 64, 64)

    def pair_copy(g):
        return remote(grads.at[g, pl.ds(other, 64)], r0.at[g], g, S0, partner)

    def s1_copy(g, k):
        return remote(s1_send.at[g, k - 1], s1_recv.at[g, k - 1], g, S1 + k - 1, peer1(k))

    def s2_copy(g, k):
        return remote(s2_send.at[g, k - 1], s2_recv.at[g, k - 1], g, S2 + k - 1, peer2(k))

    def s3_copy(g, k):
        return remote(s2_buf.at[g, (cz + k) % nz], s3_recv.at[g, k - 1], g, S3 + k - 1, peerz(k))

    def a3_copy(g, k, wait):
        at = (cz + (nz - k)) % nz if wait else cz
        ref = ag.at[g, core, c1, c2, pl.ds(at * t3, t3)]
        return remote(ref, ref, g, A3 + k - 1, peerz(k))

    def a2_copy(g, k, wait):
        at = (c2 + (n2 - k)) % n2 if wait else c2
        ref = ag.at[g, core, c1, at, pl.ds(0, t2)]
        return remote(ref, ref, g, A2 + k - 1, peer2(k))

    def a1_copy(g, k, wait):
        at = (c1 + (n1 - k)) % n1 if wait else c1
        ref = ag.at[g, core, at, :, pl.ds(0, t2)]
        return remote(ref, ref, g, A1 + k - 1, peer1(k))

    def a0_copy(g, wait):
        ref = ag.at[g, 1 - core if wait else core, :, :, pl.ds(0, t2)]
        return remote(ref, ref, g, A0, partner)

    def chip_rows(g, j):
        here = pl.multiple_of(j * r1, r1)
        return grads[g, pl.ds(mine + here, r1), :] + r0[g, pl.ds(here, r1), :]

    def scatter1(g):
        pair_copy(g).wait_recv()
        for k in range(1, n1):
            s1_send[g, k - 1] = chip_rows(g, (c1 + k) % n1).astype(jnp.bfloat16)
            s1_copy(g, k).start()

    def scatter2(g):
        total = chip_rows(g, c1)
        for k in range(1, n1):
            s1_copy(g, k).wait_recv()
            total = total + s1_recv[g, k - 1].astype(jnp.float32)
        for j in range(n2):
            for t in range(t2):
                tap = j * t2 + t
                if tap < TAPS:
                    s1_buf[g, j, t] = total[:, tap * C:(tap + 1) * C]
                else:
                    s1_buf[g, j, t] = jnp.zeros((r1, C), jnp.float32)
        for k in range(1, n2):
            s2_send[g, k - 1] = s1_buf[g, (c2 + k) % n2].astype(jnp.bfloat16)
            s2_copy(g, k).start()

    def scatter3(g):
        total = s1_buf[g, c2]
        for k in range(1, n2):
            s2_copy(g, k).wait_recv()
            total = total + s2_recv[g, k - 1].astype(jnp.float32)
        for t in range(plan.slots):
            part = total[t] if t < t2 else jnp.zeros((r1, C), jnp.float32)
            s2_buf[g, t // t3, t % t3] = part
        for k in range(1, nz):
            s3_copy(g, k).start()

    def gather3(g):
        total = s2_buf[g, cz]
        for k in range(1, nz):
            s3_copy(g, k).wait_recv()
            total = total + s3_recv[g, k - 1]
        ag[g, core, c1, c2, pl.ds(cz * t3, t3)] = (total * UNSCALE).astype(jnp.bfloat16)
        for k in range(1, nz):
            a3_copy(g, k, False).start()

    def gather2(g):
        for k in range(1, nz):
            a3_copy(g, k, True).wait_recv()
        for k in range(1, n2):
            a2_copy(g, k, False).start()

    def gather1(g):
        for k in range(1, n2):
            a2_copy(g, k, True).wait_recv()
        for k in range(1, n1):
            a1_copy(g, k, False).start()

    def gather0(g):
        for k in range(1, n1):
            a1_copy(g, k, True).wait_recv()
        a0_copy(g, False).start()

    def unpack(g, half, out):
        def body(n, carry):
            first = (half * 64 + n * r1) * TAPS
            for tap in range(TAPS):
                out[pl.ds(first + tap, r1, stride=TAPS), :] = (
                    ag[g, half, n, tap // t2, tap % t2].astype(jnp.float32)
                )
            return carry

        lax.fori_loop(0, n1, body, 0)

    corr(hid_t, st_g, grads.at[0])
    pair_copy(0).start()
    halo_wait(*args_b)
    for d in DIRS:
        fill_halo(d, pad_p, recv_b, OFFS[INDEX[d]])
    build(pad_p, st_p, True)
    scatter1(0)
    corr(in_t, st_p, grads.at[1])
    pair_copy(1).start()
    scatter2(0)
    scatter1(1)
    result = conv_back(st_p, w1r)
    fg_ref[...] = ((cot[...].astype(jnp.float32) * keep + result) * keep).astype(jnp.bfloat16)
    scatter3(0)
    scatter2(1)
    gather3(0)
    scatter3(1)
    gather2(0)
    gather3(1)
    gather1(0)
    gather2(1)
    gather0(0)
    gather1(1)
    unpack(0, core, g2_ref)
    gather0(1)
    a0_copy(0, True).wait_recv()
    unpack(0, 1 - core, g2_ref)
    unpack(1, core, g1_ref)
    a0_copy(1, True).wait_recv()
    unpack(1, 1 - core, g1_ref)

    halo_sent(*args_a)
    halo_sent(*args_b)
    for g in range(2):
        pair_copy(g).wait_send()
        for k in range(1, n1):
            s1_copy(g, k).wait_send()
            a1_copy(g, k, False).wait_send()
        for k in range(1, n2):
            s2_copy(g, k).wait_send()
            a2_copy(g, k, False).wait_send()
        for k in range(1, nz):
            s3_copy(g, k).wait_send()
            a3_copy(g, k, False).wait_send()
        a0_copy(g, False).wait_send()


def on_device(plan, features, tile_mask, w_first, w_second, cotangent):
    n1, n2, nz, r1, t2, t3 = plan.nx, plan.ny, plan.nz, plan.r1, plan.t2, plan.t3
    f32, bf16 = jnp.float32, jnp.bfloat16
    rows = TAPS * C
    copies = 2 * (n1 - 1 + n2 - 1 + nz - 1 + 1)
    pad = pltpu.VMEM(((T + 2) * (T + 2) * ZS, C), f32)
    stacked = pltpu.VMEM((T + 2, 64, K3), bf16)
    halo_a = pltpu.VMEM((2 * TILES, 8, C), bf16)
    halo_b = pltpu.VMEM((TILES, 8, C), bf16)
    dma = pltpu.SemaphoreType.DMA
    any_spec = pl.BlockSpec(memory_space=pl.ANY)
    vmem_spec = pl.BlockSpec(memory_space=pltpu.VMEM)
    scratch = [
        pltpu.VMEM((512, C), bf16), pltpu.VMEM((512, C), bf16),
        pltpu.VMEM((rows, C), bf16), pltpu.VMEM((rows, C), bf16), pltpu.VMEM((rows, C), f32),
        pltpu.VMEM((C, rows), bf16), pltpu.VMEM((C, rows), bf16), pltpu.VMEM((rows, C), bf16),
        pad, pad, pad, stacked, stacked, stacked,
        halo_a, halo_a, halo_b, halo_b,
        pltpu.VMEM((C, 512), bf16), pltpu.VMEM((C, 512), bf16), pltpu.VMEM((8, C), f32),
        pltpu.VMEM((2, C, rows), f32), pltpu.VMEM((2, 64, rows), f32),
        pltpu.VMEM((2, n1 - 1, r1, rows), bf16), pltpu.VMEM((2, n1 - 1, r1, rows), bf16),
        pltpu.VMEM((2, n2, t2, r1, C), f32),
        pltpu.VMEM((2, n2 - 1, t2, r1, C), bf16), pltpu.VMEM((2, n2 - 1, t2, r1, C), bf16),
        pltpu.VMEM((2, nz, t3, r1, C), f32), pltpu.VMEM((2, nz - 1, t3, r1, C), f32),
        pltpu.VMEM((2, 2, n1, n2, plan.slots, r1, C), bf16),
        dma((4,)), dma((26,)), dma((26,)), dma((26,)), dma((26,)),
        dma((2, copies)), dma((2, copies)),
    ]
    feature_grad, grad_first, grad_second = pl.pallas_call(
        functools.partial(kernel, plan),
        out_shape=(
            jax.ShapeDtypeStruct((512, C), bf16),
            jax.ShapeDtypeStruct((rows, C), f32),
            jax.ShapeDtypeStruct((rows, C), f32),
        ),
        in_specs=[pl.BlockSpec(memory_space=pltpu.SMEM)] + [any_spec] * 4,
        out_specs=(vmem_spec,) * 3,
        scratch_shapes=scratch,
        compiler_params=pltpu.CompilerParams(collective_id=0, has_side_effects=True),
        name="block_backward",
    )(tile_mask, features[0], cotangent[0], w_first, w_second)
    return grad_first, grad_second, feature_grad[None]


def solution(mesh):
    blocks = mesh.shape["blk"]
    ny = nx = 4 if blocks >= 16 else 2
    plan = Plan(blocks // (nx * ny), nx, ny)
    in_specs = (P("dp", "blk", None), P("dp", "blk"), P(), P(), P("dp", "blk", None))
    out_specs = (P(), P(), P("dp", "blk", None))
    return jax.shard_map(
        functools.partial(on_device, plan), mesh=mesh, in_specs=in_specs, out_specs=out_specs, check_vma=False
    )
```

time: 1230 us -> 69.3 us (0.06)
  waiting for transfers between devices: 708 us -> 0 us
  starting transfers between devices: 377 us -> 0 us
  local copies, waits for them, and re-layouts: 88.6 us -> 4.8 us
  Pallas kernels: 0 us -> 63.1 us
  between operations: 17.8 us -> 1.3 us
  matrix products: 15.2 us -> 0 us
  other arithmetic: 13.3 us -> 0 us
    psum x1 -> x0, waiting for transfers between devices: 382 us -> none  [reduce_rows(): return lax.psum(term, ('dp', 'blk'))]
    ppermute x104 -> x0, starting transfers between devices: 377 us -> none  [shifted(): lax.ppermute(value, axis, [(source, source + steps) for source in range(l...]
    ppermute x104 -> x0, waiting for transfers between devices: 325 us -> none  [shifted(): lax.ppermute(value, axis, [(source, source + steps) for source in range(l...]
    pallas_call x0 -> x1, Pallas kernels: none -> 63.1 us  [on_device(): pl.pallas_call(functools.partial(kernel, plan), out_shape=(jax.ShapeDtype...]
    dynamic_update_slice x104 -> x0, local copies, waits for them, and re-layouts: 36 us -> none  [direct_rims(): lax.dynamic_update_slice(padded, arrived, (starts[0], starts[1], starts[2...]
    slice x48 -> x0, local copies, waits for them, and re-layouts: 24.1 us -> none  [the longest x40 19.4 us: direct_rims(): sliced = lax.slice_in_dim(sliced, 0, 1, axis=axis_pos)]
    dot_general x45 -> x0, matrix products: 15.2 us -> none  [the longest x27 9.52 us: convolve(): jnp.dot(slab_rows, kernel[step_x, step_y], preferred_element_type=jnp.flo...]
  transfers between devices with their start and end apart: 105 -> 0, of which waited for: 90 -> 0; matrix products, arithmetic and copies ran while one was open for 7% -> 0% of each run, Pallas kernels for 0% -> 0%
where the time goes in v1:
time: 69.3 us; the launch traced here: 69.2 us
  Pallas kernels  63.1 us (91%)
  local copies, waits for them, and re-layouts  4.8 us (7%)
  between operations  1.3 us (2%)
    pallas_call x1, Pallas kernels, on_device(): pl.pallas_call(functools.partial(kernel, plan), out_shape=(jax.ShapeDtype...  63.1 us
    unnamed x7, local copies, waits for them, and re-layouts  4.8 us

profile of v1, /device:TPU:1, one launch (start us, length us, event | category | flops | bytes accessed | tf_op | source)
XLA Modules:
  0.0 69.2 jit_solution(10302939819097526627)
XLA Ops:
  1.3 63.1 %block_backward.1 = (bf16[512,128]{1,0:T(8,128)(2,1)}, f32[3456,128]{1,0:T(8,128)}, f32[3456,128]{1,0:T(8,128)}) custom-call(s32[1,1]{1,0:T(1,128)S(6)} %copy.11.mask_ref, bf16[512,128]{1,0:T(8,128)(2,1)} %bitcast.3, bf16[512,128]{1,0:T(8,128)(2,1)} %bitcast.4, bf16[3456,128]{1,0:T(8,128)(2,1)} %w1_hbm.1, bf16[3456,128]{1,0:T(8,128)(2,1)} %w2_hbm.1), custom_call_target="tpu_custom_call" | custom-call | tf_op jit(solution)/shard_map/block_backward/pallas_call | solution.py:477
  64.4 0.0 copy-start
  64.4 2.9 %copy.12 = f32[3456,128]{1,0:T(8,128)} copy(f32[3456,128]{1,0:T(8,128)} %get-tuple-element.12) | data formatting | bytes 3538944
  67.3 0.0 copy-done
  67.3 0.0 copy-start.1
  67.3 1.2 %copy.13 = f32[3456,128]{1,0:T(8,128)} copy(f32[3456,128]{1,0:T(8,128)S(1)} %copy-done) | data formatting | bytes 3538944
  68.5 0.0 copy-done.1
  68.5 0.7 copy.14
Async XLA Ops:
  64.4 2.9 %copy-start = (f32[3456,128]{1,0:T(8,128)S(1)}, f32[3456,128]{1,0:T(8,128)}, u32[]{:S(2)}) copy-start(f32[3456,128]{1,0:T(8,128)} %get-tuple-element.13) | copy-start | bytes 5308420
  67.3 1.2 %copy-start.1 = (bf16[512,128]{1,0:T(8,128)(2,1)S(1)}, bf16[512,128]{1,0:T(8,128)(2,1)}, u32[]{:S(2)}) copy-start(bf16[512,128]{1,0:T(8,128)(2,1)} %get-tuple-element.8) | copy-start | bytes 393220

commit v2 on v1

--- a/solution.py
+++ b/solution.py
@@ -63,23 +63,21 @@
         self.n1 = nx
         self.r1 = 64 // nx
         self.t2 = -(-TAPS // ny)
-        self.t3 = -(-self.t2 // nz)
-        self.slots = self.t3 * nz
 
 
 def kernel(
     plan,
     mask_ref, feat_hbm, cot_hbm, w1_hbm, w2_hbm,
-    fg_ref, g1_ref, g2_ref,
+    fg_ref, ag_out,
     feat, cot, w1, w2, wf, w1r, w2r, b1,
     pad_i, pad_g, pad_p, st_i, st_g, st_p,
     send_a, recv_a, send_b, recv_b,
-    in_t, hid_t, pg_own,
-    grads, r0, s1_send, s1_recv, s1_buf, s2_send, s2_recv, s2_buf, s3_recv, ag,
+    pg_t, hid_t,
+    grads, r0, s1_send, s1_recv, s1_own, s2_send, s2_recv, z_all, ag,
     load_sem, ha_send, ha_recv, hb_send, hb_recv, red_send, red_recv,
 ):
     nz, nx, ny = plan.nz, plan.nx, plan.ny
-    n1, n2, r1, t2, t3 = nx, ny, plan.r1, plan.t2, plan.t3
+    n1, n2, r1, t2 = nx, ny, plan.r1, plan.t2
     core = lax.axis_index("dp")
     blk = lax.axis_index("blk")
     cz = blk // (nx * ny)
@@ -223,7 +221,8 @@
     args_a = (send_a, recv_a, ha_send, ha_recv, 2)
     halo_start(*args_a)
 
-    in_t[...] = inputs.T.astype(jnp.bfloat16)
+    for g in range(2):
+        grads[g, n2 - 1, :, (TAPS - (n2 - 1) * t2) * C:] = jnp.zeros((C, (n2 * t2 - TAPS) * C), jnp.float32)
     loads[2].wait()
     loads[3].wait()
     for w, arranged, stacked in ((w1, w1r, b1), (w2, w2r, None)):
@@ -258,12 +257,6 @@
             total = term if total is None else total + term
         return total
 
-    def corr(lhs_t, stacked, out):
-        for a in range(3):
-            out[:, a * K3:(a + 1) * K3] = jnp.dot(
-                lhs_t[...], slab(stacked, 2 - a), preferred_element_type=jnp.float32
-            )
-
     pre_act = None
     for a in range(3):
         term = jnp.dot(slab(st_i, a), b1[a * K3:(a + 1) * K3, :], preferred_element_type=jnp.float32)
@@ -273,184 +266,225 @@
     hid_t[...] = (pre_act * sigma * keep).T.astype(jnp.bfloat16)
     pre_grad = back * sigma * (1.0 + pre_act * (1.0 - sigma)) * keep
     fill_own(pad_p, pre_grad)
+    pg_t[...] = pre_grad.T.astype(jnp.bfloat16)
+
+    names = dict(pair=n2, s1=3 * n2, s2=n2 - 1, zs=nz - 1, a2=n2 - 1, a1=3 * n2, a0=n1)
+    first_of = {}
+    total_sems = 0
+    for name, size in names.items():
+        first_of[name] = total_sems
+        total_sems += size
+    started = []
+
+    def remote(src, dst, g, name, n, peer):
+        at = first_of[name] + n
+        return pltpu.make_async_remote_copy(
+            src_ref=src, dst_ref=dst, send_sem=red_send.at[g, at], recv_sem=red_recv.at[g, at],
+            device_id=peer, device_id_type=MESH,
+        )
+
+    def go(copy):
+        copy.start()
+        started.append(copy)
+
+    mine = pl.multiple_of(core * 64, 64)
+    other = pl.multiple_of(64 - core * 64, 64)
+    firsts = ((c2, c1), (c1, c2))
+    hop1 = (peer2, peer1)
+    hop2 = (peer1, peer2)
+
+    def chunk(g, i):
+        return (firsts[g][1] + 1 + i) % n2
+
+    def pair_copy(g, j):
+        return remote(grads.at[g, j, pl.ds(other, 64)], r0.at[g, j], g, "pair", j, partner)
+
+    def chip(g, j, block):
+        here = pl.multiple_of(block % n1 * r1, r1)
+        return grads[g, j, pl.ds(mine + here, r1), :] + r0[g, j, pl.ds(here, r1), :]
+
+    def s1_copy(g, i, k):
+        return remote(s1_send.at[g, i, k - 1], s1_recv.at[g, i, k - 1], g, "s1", 3 * i + k - 1, hop1[g](k))
+
+    def s2_copy(g, k):
+        return remote(s2_send.at[g, k - 1], s2_recv.at[g, k - 1], g, "s2", k - 1, hop2[g](k))
+
+    def z_copy(g, k, wait):
+        ref = z_all.at[g, (cz + (nz - k)) % nz if wait else cz]
+        return remote(ref, ref, g, "zs", k - 1, peerz(k))
+
+    def a2_copy(g, k, wait):
+        b, j = firsts[g]
+        ref = ag.at[g, core, b, (j + (n2 - k)) % n2 if wait else j]
+        return remote(ref, ref, g, "a2", k - 1, hop2[g](k))
+
+    def a1_copy(g, m, k, wait):
+        b, j = firsts[g]
+        ref = ag.at[g, core, (b + (n1 - k)) % n1 if wait else b, (j + (n2 - m)) % n2]
+        return remote(ref, ref, g, "a1", 3 * m + k - 1, hop1[g](k))
+
+    def a0_copy(g, n, wait):
+        ref = ag.at[g, 1 - core if wait else core, (firsts[g][1 if wait else 0] + (n1 - n)) % n1]
+        return remote(ref, ref, g, "a0", n, partner)
+
+    def corr(g, lhs_t, slab_of):
+        sent = 0
+        for a in range(3):
+            part = jnp.dot(lhs_t[...], slab_of(a), preferred_element_type=jnp.float32)
+            for n in range(9):
+                tap = 9 * a + n
+                at = tap % t2 * C
+                grads[g, tap // t2, :, at:at + C] = part[:, n * C:(n + 1) * C]
+            while sent < n2 and min((sent + 1) * t2, TAPS) <= 9 * (a + 1):
+                go(pair_copy(g, sent))
+                sent += 1
+
+    far_first = (2, 1, 3)
+
+    def scatter1(g):
+        for i in range(n2):
+            j = chunk(g, i)
+            pair_copy(g, j).wait_recv()
+            for k in far_first:
+                s1_send[g, i, k - 1] = chip(g, j, firsts[g][0] + k).astype(jnp.bfloat16)
+                go(s1_copy(g, i, k))
+
+    def scatter2(g):
+        for i in range(n2):
+            total = chip(g, chunk(g, i), firsts[g][0])
+            for k in range(1, n1):
+                s1_copy(g, i, k).wait_recv()
+                total = total + s1_recv[g, i, k - 1].astype(jnp.float32)
+            if i < n2 - 1:
+                s2_send[g, i] = total
+                go(s2_copy(g, i + 1))
+            else:
+                s1_own[g] = total
+
+    z_order = (4, 3, 5, 2, 6, 1, 7)
+
+    def scatter3(g):
+        total = s1_own[g]
+        for k in range(1, n2):
+            s2_copy(g, k).wait_recv()
+            total = total + s2_recv[g, k - 1]
+        z_all[g, cz] = total.astype(jnp.bfloat16)
+        for k in z_order:
+            go(z_copy(g, k, False))
+
+    def gather2(g):
+        for k in reversed(z_order):
+            z_copy(g, k, True).wait_recv()
+        total = z_all[g, 0].astype(jnp.float32)
+        for z in range(1, nz):
+            total = total + z_all[g, z].astype(jnp.float32)
+        b, j = firsts[g]
+        ag[g, core, b, j] = (total * UNSCALE).astype(jnp.bfloat16)
+        for k in far_first:
+            go(a2_copy(g, k, False))
+        for k in far_first:
+            go(a1_copy(g, 0, k, False))
+
+    def gather1(g):
+        for m in (1, 3, 2):
+            a2_copy(g, m, True).wait_recv()
+            for k in far_first:
+                go(a1_copy(g, m, k, False))
+        go(a0_copy(g, 0, False))
+
+    def gather0(g):
+        for k in (1, 3, 2):
+            for m in (0, 1, 3, 2):
+                a1_copy(g, m, k, True).wait_recv()
+            go(a0_copy(g, k, False))
+
+    def finish(g):
+        for n in (0, 1, 3, 2):
+            a0_copy(g, n, True).wait_recv()
+        done = pltpu.make_async_copy(ag.at[g], ag_out.at[g], load_sem.at[4 + g])
+        done.start()
+        return done
+
+    corr(1, pg_t, lambda a: slab(st_i, a))
+    corr(0, hid_t, lambda a: slab(st_g, 2 - a))
+    scatter1(1)
+    scatter1(0)
     for d in DIRS:
         stage(d, pad_p, send_b, OFFS[INDEX[d]])
     args_b = (send_b, recv_b, hb_send, hb_recv, 1)
     halo_start(*args_b)
-
-    def remote(src, dst, g, n, peer):
-        return pltpu.make_async_remote_copy(
-            src_ref=src, dst_ref=dst, send_sem=red_send.at[g, n], recv_sem=red_recv.at[g, n],
-            device_id=peer, device_id_type=MESH,
-        )
-
-    S0, S1 = 0, 1
-    S2 = S1 + n1 - 1
-    S3 = S2 + n2 - 1
-    A3 = S3 + nz - 1
-    A2 = A3 + nz - 1
-    A1 = A2 + n2 - 1
-    A0 = A1 + n1 - 1
-    mine = pl.multiple_of(core * 64, 64)
-    other = pl.multiple_of(64 - core * 64, 64)
-
-    def pair_copy(g):
-        return remote(grads.at[g, pl.ds(other, 64)], r0.at[g], g, S0, partner)
-
-    def s1_copy(g, k):
-        return remote(s1_send.at[g, k - 1], s1_recv.at[g, k - 1], g, S1 + k - 1, peer1(k))
-
-    def s2_copy(g, k):
-        return remote(s2_send.at[g, k - 1], s2_recv.at[g, k - 1], g, S2 + k - 1, peer2(k))
-
-    def s3_copy(g, k):
-        return remote(s2_buf.at[g, (cz + k) % nz], s3_recv.at[g, k - 1], g, S3 + k - 1, peerz(k))
-
-    def a3_copy(g, k, wait):
-        at = (cz + (nz - k)) % nz if wait else cz
-        ref = ag.at[g, core, c1, c2, pl.ds(at * t3, t3)]
-        return remote(ref, ref, g, A3 + k - 1, peerz(k))
-
-    def a2_copy(g, k, wait):
-        at = (c2 + (n2 - k)) % n2 if wait else c2
-        ref = ag.at[g, core, c1, at, pl.ds(0, t2)]
-        return remote(ref, ref, g, A2 + k - 1, peer2(k))
-
-    def a1_copy(g, k, wait):
-        at = (c1 + (n1 - k)) % n1 if wait else c1
-        ref = ag.at[g, core, at, :, pl.ds(0, t2)]
-        return remote(ref, ref, g, A1 + k - 1, peer1(k))
-
-    def a0_copy(g, wait):
-        ref = ag.at[g, 1 - core if wait else core, :, :, pl.ds(0, t2)]
-        return remote(ref, ref, g, A0, partner)
-
-    def chip_rows(g, j):
-        here = pl.multiple_of(j * r1, r1)
-        return grads[g, pl.ds(mine + here, r1), :] + r0[g, pl.ds(here, r1), :]
-
-    def scatter1(g):
-        pair_copy(g).wait_recv()
-        for k in range(1, n1):
-            s1_send[g, k - 1] = chip_rows(g, (c1 + k) % n1).astype(jnp.bfloat16)
-            s1_copy(g, k).start()
-
-    def scatter2(g):
-        total = chip_rows(g, c1)
-        for k in range(1, n1):
-            s1_copy(g, k).wait_recv()
-            total = total + s1_recv[g, k - 1].astype(jnp.float32)
-        for j in range(n2):
-            for t in range(t2):
-                tap = j * t2 + t
-                if tap < TAPS:
-                    s1_buf[g, j, t] = total[:, tap * C:(tap + 1) * C]
-                else:
-                    s1_buf[g, j, t] = jnp.zeros((r1, C), jnp.float32)
-        for k in range(1, n2):
-            s2_send[g, k - 1] = s1_buf[g, (c2 + k) % n2].astype(jnp.bfloat16)
-            s2_copy(g, k).start()
-
-    def scatter3(g):
-        total = s1_buf[g, c2]
-        for k in range(1, n2):
-            s2_copy(g, k).wait_recv()
-            total = total + s2_recv[g, k - 1].astype(jnp.float32)
-        for t in range(plan.slots):
-            part = total[t] if t < t2 else jnp.zeros((r1, C), jnp.float32)
-            s2_buf[g, t // t3, t % t3] = part
-        for k in range(1, nz):
-            s3_copy(g, k).start()
-
-    def gather3(g):
-        total = s2_buf[g, cz]
-        for k in range(1, nz):
-            s3_copy(g, k).wait_recv()
-            total = total + s3_recv[g, k - 1]
-        ag[g, core, c1, c2, pl.ds(cz * t3, t3)] = (total * UNSCALE).astype(jnp.bfloat16)
-        for k in range(1, nz):
-            a3_copy(g, k, False).start()
-
-    def gather2(g):
-        for k in range(1, nz):
-            a3_copy(g, k, True).wait_recv()
-        for k in range(1, n2):
-            a2_copy(g, k, False).start()
-
-    def gather1(g):
-        for k in range(1, n2):
-            a2_copy(g, k, True).wait_recv()
-        for k in range(1, n1):
-            a1_copy(g, k, False).start()
-
-    def gather0(g):
-        for k in range(1, n1):
-            a1_copy(g, k, True).wait_recv()
-        a0_copy(g, False).start()
-
-    def unpack(g, half, out):
-        def body(n, carry):
-            first = (half * 64 + n * r1) * TAPS
-            for tap in range(TAPS):
-                out[pl.ds(first + tap, r1, stride=TAPS), :] = (
-                    ag[g, half, n, tap // t2, tap % t2].astype(jnp.float32)
-                )
-            return carry
-
-        lax.fori_loop(0, n1, body, 0)
-
-    corr(hid_t, st_g, grads.at[0])
-    pair_copy(0).start()
+    scatter2(1)
+    scatter2(0)
     halo_wait(*args_b)
     for d in DIRS:
         fill_halo(d, pad_p, recv_b, OFFS[INDEX[d]])
     build(pad_p, st_p, True)
-    scatter1(0)
-    corr(in_t, st_p, grads.at[1])
-    pair_copy(1).start()
-    scatter2(0)
-    scatter1(1)
+    scatter3(1)
+    scatter3(0)
     result = conv_back(st_p, w1r)
     fg_ref[...] = ((cot[...].astype(jnp.float32) * keep + result) * keep).astype(jnp.bfloat16)
-    scatter3(0)
-    scatter2(1)
-    gather3(0)
-    scatter3(1)
+    gather2(1)
     gather2(0)
-    gather3(1)
+    gather1(1)
     gather1(0)
-    gather2(1)
+    gather0(1)
     gather0(0)
-    gather1(1)
-    unpack(0, core, g2_ref)
-    gather0(1)
-    a0_copy(0, True).wait_recv()
-    unpack(0, 1 - core, g2_ref)
-    unpack(1, core, g1_ref)
-    a0_copy(1, True).wait_recv()
-    unpack(1, 1 - core, g1_ref)
+    done1 = finish(1)
+    done0 = finish(0)
 
     halo_sent(*args_a)
     halo_sent(*args_b)
-    for g in range(2):
-        pair_copy(g).wait_send()
-        for k in range(1, n1):
-            s1_copy(g, k).wait_send()
-            a1_copy(g, k, False).wait_send()
-        for k in range(1, n2):
-            s2_copy(g, k).wait_send()
-            a2_copy(g, k, False).wait_send()
-        for k in range(1, nz):
-            s3_copy(g, k).wait_send()
-            a3_copy(g, k, False).wait_send()
-        a0_copy(g, False).wait_send()
+    for copy in started:
+        copy.wait_send()
+    done1.wait()
+    done0.wait()
+
+
+def unpack_kernel(plan, ag_hbm, fg_hbm, g1_hbm, g2_hbm, fg_out, ag, fg, g1, g2, sems):
+    n1, r1, t2 = plan.nx, plan.r1, plan.t2
+    rows = r1 * TAPS
+    loads = [
+        pltpu.make_async_copy(src, dst, sems.at[n])
+        for n, (src, dst) in enumerate(((ag_hbm.at[0], ag.at[0]), (ag_hbm.at[1], ag.at[1]), (fg_hbm, fg)))
+    ]
+    for copy in loads:
+        copy.start()
+    stores = []
+
+    def put(src, dst):
+        copy = pltpu.make_async_copy(src, dst, sems.at[3 + len(stores)])
+        copy.start()
+        stores.append(copy)
+
+    loads[0].wait()
+    for half in range(2):
+        for block in range(n1):
+            first = (half * n1 + block) * rows
+            for tap in range(TAPS):
+                lanes = pl.ds(tap % t2 * C, C)
+                g2[pl.ds(first + tap, r1, stride=TAPS), :] = (
+                    ag[0, half, block, tap // t2, :, lanes].astype(jnp.float32)
+                )
+            put(g2.at[pl.ds(first, rows)], g2_hbm.at[pl.ds(first, rows)])
+    loads[2].wait()
+    put(fg, fg_out)
+    loads[1].wait()
+    for tap in range(TAPS):
+        block = ag[1, :, :, tap // t2, :, pl.ds(tap % t2 * C, C)].reshape(C, C)
+        g1[pl.ds(tap, C, stride=TAPS), :] = block.astype(jnp.float32).T
+    put(g1, g1_hbm)
+    for copy in stores:
+        copy.wait()
 
 
 def on_device(plan, features, tile_mask, w_first, w_second, cotangent):
-    n1, n2, nz, r1, t2, t3 = plan.nx, plan.ny, plan.nz, plan.r1, plan.t2, plan.t3
+    n1, n2, nz, r1, t2 = plan.nx, plan.ny, plan.nz, plan.r1, plan.t2
     f32, bf16 = jnp.float32, jnp.bfloat16
     rows = TAPS * C
-    copies = 2 * (n1 - 1 + n2 - 1 + nz - 1 + 1)
+    copies = 7 * n2 + n1 + 2 * (n2 - 1) + nz - 1
+    gathered = (2, 2, n1, n2, r1, t2 * C)
+    s1_buf = pltpu.VMEM((2, n2, n1 - 1, r1, t2 * C), bf16)
+    s2_buf = pltpu.VMEM((2, n2 - 1, r1, t2 * C), f32)
     pad = pltpu.VMEM(((T + 2) * (T + 2) * ZS, C), f32)
     stacked = pltpu.VMEM((T + 2, 64, K3), bf16)
     halo_a = pltpu.VMEM((2 * TILES, 8, C), bf16)
@@ -464,29 +498,38 @@
         pltpu.VMEM((C, rows), bf16), pltpu.VMEM((C, rows), bf16), pltpu.VMEM((rows, C), bf16),
         pad, pad, pad, stacked, stacked, stacked,
         halo_a, halo_a, halo_b, halo_b,
-        pltpu.VMEM((C, 512), bf16), pltpu.VMEM((C, 512), bf16), pltpu.VMEM((8, C), f32),
-        pltpu.VMEM((2, C, rows), f32), pltpu.VMEM((2, 64, rows), f32),
-        pltpu.VMEM((2, n1 - 1, r1, rows), bf16), pltpu.VMEM((2, n1 - 1, r1, rows), bf16),
-        pltpu.VMEM((2, n2, t2, r1, C), f32),
-        pltpu.VMEM((2, n2 - 1, t2, r1, C), bf16), pltpu.VMEM((2, n2 - 1, t2, r1, C), bf16),
-        pltpu.VMEM((2, nz, t3, r1, C), f32), pltpu.VMEM((2, nz - 1, t3, r1, C), f32),
-        pltpu.VMEM((2, 2, n1, n2, plan.slots, r1, C), bf16),
-        dma((4,)), dma((26,)), dma((26,)), dma((26,)), dma((26,)),
+        pltpu.VMEM((C, 512), bf16), pltpu.VMEM((C, 512), bf16),
+        pltpu.VMEM((2, n2, C, t2 * C), f32), pltpu.VMEM((2, n2, 64, t2 * C), f32),
+        s1_buf, s1_buf, pltpu.VMEM((2, r1, t2 * C), f32), s2_buf, s2_buf,
+        pltpu.VMEM((2, nz, r1, t2 * C), bf16),
+        pltpu.VMEM(gathered, bf16),
+        dma((6,)), dma((26,)), dma((26,)), dma((26,)), dma((26,)),
         dma((2, copies)), dma((2, copies)),
     ]
-    feature_grad, grad_first, grad_second = pl.pallas_call(
+    partial_fg, partial_ag = pl.pallas_call(
         functools.partial(kernel, plan),
-        out_shape=(
-            jax.ShapeDtypeStruct((512, C), bf16),
-            jax.ShapeDtypeStruct((rows, C), f32),
-            jax.ShapeDtypeStruct((rows, C), f32),
-        ),
+        out_shape=(jax.ShapeDtypeStruct((512, C), bf16), jax.ShapeDtypeStruct(gathered, bf16)),
         in_specs=[pl.BlockSpec(memory_space=pltpu.SMEM)] + [any_spec] * 4,
-        out_specs=(vmem_spec,) * 3,
+        out_specs=(vmem_spec, any_spec),
         scratch_shapes=scratch,
         compiler_params=pltpu.CompilerParams(collective_id=0, has_side_effects=True),
         name="block_backward",
     )(tile_mask, features[0], cotangent[0], w_first, w_second)
+    grad_first, grad_second, feature_grad = pl.pallas_call(
+        functools.partial(unpack_kernel, plan),
+        out_shape=(
+            jax.ShapeDtypeStruct((rows, C), f32),
+            jax.ShapeDtypeStruct((rows, C), f32),
+            jax.ShapeDtypeStruct((512, C), bf16),
+        ),
+        in_specs=[any_spec] * 2,
+        out_specs=(any_spec,) * 3,
+        scratch_shapes=[
+            pltpu.VMEM(gathered, bf16), pltpu.VMEM((512, C), bf16),
+            pltpu.VMEM((rows, C), f32), pltpu.VMEM((rows, C), f32), dma((3 + 2 * n1 + 2,)),
+        ],
+        name="unpack",
+    )(partial_ag, partial_fg)
     return grad_first, grad_second, feature_grad[None]
 
 

time: 69.3 us -> 59.7 us (0.86)
  Pallas kernels: 63.1 us -> 58.3 us
  local copies, waits for them, and re-layouts: 4.8 us -> 0 us
    pallas_call x1, Pallas kernels: 63.1 us -> 55.2 us  [on_device(): pl.pallas_call(functools.partial(kernel, plan), out_shape=(jax.ShapeDtype...]
    unnamed x7 -> x0, local copies, waits for them, and re-layouts: 4.8 us -> none
    pallas_call x0 -> x1, Pallas kernels: none -> 3.14 us  [on_device(): pl.pallas_call(functools.partial(unpack_kernel, plan), out_shape=(jax.Sha...]
where the time goes in v2:
time: 59.7 us; the launch traced here: 59.6 us
  Pallas kernels  58.3 us (98%)
  between operations  1.28 us (2%)
    pallas_call x1, Pallas kernels, on_device(): pl.pallas_call(functools.partial(kernel, plan), out_shape=(jax.ShapeDtype...  55.2 us
    pallas_call x1, Pallas kernels, on_device(): pl.pallas_call(functools.partial(unpack_kernel, plan), out_shape=(jax.Sha...  3.14 us

profile of v2, /device:TPU:1, one launch (start us, length us, event | category | flops | bytes accessed | tf_op | source)
XLA Modules:
  0.0 59.6 jit_solution(1547674933892527991)
XLA Ops:
  1.3 55.2 %block_backward.1 = (bf16[512,128]{1,0:T(8,128)(2,1)}, bf16[2,2,4,4,16,896]{5,4,3,2,1,0:T(8,128)(2,1)}) custom-call(s32[1,1]{1,0:T(1,128)S(6)} %copy.8.mask_ref, bf16[512,128]{1,0:T(8,128)(2,1)} %bitcast.3, bf16[512,128]{1,0:T(8,128)(2,1)} %bitcast.4, bf16[3456,128]{1,0:T(8,128)(2,1)} %w1_hbm.1, bf16[3456,128]{1,0:T(8,128)(2,1)} %w2_hbm.1), custom_call_target="tpu_custom_call" | custom-call | tf_op jit(solution)/shard_map/block_backward/pallas_call | solution.py:509
  56.5 3.1 %unpack.1 = (f32[3456,128]{1,0:T(8,128)}, f32[3456,128]{1,0:T(8,128)}, bf16[512,128]{1,0:T(8,128)(2,1)}) custom-call(bf16[2,2,4,4,16,896]{5,4,3,2,1,0:T(8,128)(2,1)} %get-tuple-element.8.ag_hbm, bf16[512,128]{1,0:T(8,128)(2,1)} %get-tuple-element.9.fg_hbm), custom_call_target="tpu_custom_call" | custom-call | tf_op jit(solution)/shard_map/unpack/pallas_call | solution.py:518

commit v3 on v2

--- a/solution.py
+++ b/solution.py
@@ -68,13 +68,13 @@
 def kernel(
     plan,
     mask_ref, feat_hbm, cot_hbm, w1_hbm, w2_hbm,
-    fg_ref, ag_out,
+    fg_out, ag_out,
     feat, cot, w1, w2, wf, w1r, w2r, b1,
     pad_i, pad_g, pad_p, st_i, st_g, st_p,
     send_a, recv_a, send_b, recv_b,
     pg_t, hid_t,
-    grads, r0, s1_send, s1_recv, s1_own, s2_send, s2_recv, z_all, ag,
-    load_sem, ha_send, ha_recv, hb_send, hb_recv, red_send, red_recv,
+    grads, r0, s1_send, s1_recv, s1_own, s2_send, s2_recv, z_all, ag, fg,
+    load_sem, out_sem, ha_sems, hb_sems, red_send, red_recv,
 ):
     nz, nx, ny = plan.nz, plan.nx, plan.ny
     n1, n2, r1, t2 = nx, ny, plan.r1, plan.t2
@@ -91,9 +91,6 @@
     for copy in loads:
         copy.start()
 
-    recv_a[...] = jnp.zeros_like(recv_a)
-    recv_b[...] = jnp.zeros_like(recv_b)
-
     step1 = ny - (ny - 1) * core
     step2 = 1 + (ny - 1) * core
     c1 = cx + (cy - cx) * core
@@ -122,23 +119,20 @@
             inside = test if inside is None else jnp.logical_and(inside, test)
         return inside
 
-    def neighbour(d):
-        return (core, blk + d[0] * (nx * ny) + d[1] * ny + d[2])
+    inside = {d: valid(d).astype(jnp.int32) for d in DIRS}
+
+    def target(d):
+        here = inside[d]
+        step = d[0] * (nx * ny) + d[1] * ny + d[2]
+        return (core + (1 - here) * (1 - 2 * core), blk + here * step)
 
     barrier = pltpu.get_barrier_semaphore()
-    count = jnp.int32(1 + (n1 - 1) + (n2 - 1) + (nz - 1))
-    peers = [partner] + [peer1(k) for k in range(1, n1)] + [peer2(k) for k in range(1, n2)]
-    peers += [peerz(k) for k in range(1, nz)]
+    peers = [target(d) for d in DIRS if sum(abs(v) for v in d) > 1]
+    peers += [peerz(k) for k in range(1, nz)] + [partner]
+    peers += [peer1(k) for k in range(1, n1)] + [peer2(k) for k in range(1, n2)]
     for peer in peers:
         pl.semaphore_signal(barrier, inc=1, device_id=peer, device_id_type=MESH)
-    for d in DIRS:
-        if sum(abs(v) for v in d) > 1:
-            here = valid(d)
-            count = count + here.astype(jnp.int32)
-
-            @pl.when(here)
-            def _():
-                pl.semaphore_signal(barrier, inc=1, device_id=neighbour(d), device_id_type=MESH)
+    count = len(peers)
 
     keep = mask_ref[0, 0].astype(jnp.float32)
 
@@ -155,37 +149,30 @@
 
     def fill_halo(d, pad, recv, base):
         for n, (start, stride, size) in enumerate(boundary_tiles(d, True)):
-            pad[rows_of(start, stride, size), :] = recv[base + n, 0:size].astype(jnp.float32)
-
-    def halo_copy(d, send, recv, send_sem, recv_sem, arrays):
-        there = opposite(d)
-        size = SIZES[INDEX[d]] * arrays
+            tile = recv[base + n, 0:size].astype(jnp.float32)
+            pad[rows_of(start, stride, size), :] = jnp.where(inside[d] > 0, tile, jnp.zeros_like(tile))
+
+    def halo_start(send, recv, sems, arrays):
+        for d in DIRS:
+            here, there = OFFS[INDEX[d]] * arrays, OFFS[INDEX[opposite(d)]] * arrays
+            size = SIZES[INDEX[d]] * arrays
+            pltpu.make_async_remote_copy(
+                src_ref=send.at[pl.ds(here, size)],
+                dst_ref=recv.at[pl.ds(here + inside[d] * (there - here), size)],
+                send_sem=sems.at[0], recv_sem=sems.at[1], device_id=target(d), device_id_type=MESH,
+            ).start()
+
+    def halo_all(send, recv, sems, arrays):
         return pltpu.make_async_remote_copy(
-            src_ref=send.at[pl.ds(OFFS[INDEX[d]] * arrays, size)],
-            dst_ref=recv.at[pl.ds(OFFS[INDEX[there]] * arrays, size)],
-            send_sem=send_sem.at[INDEX[d]],
-            recv_sem=recv_sem.at[INDEX[there]],
-            device_id=neighbour(d),
-            device_id_type=MESH,
+            src_ref=send, dst_ref=recv, send_sem=sems.at[0], recv_sem=sems.at[1],
+            device_id=partner, device_id_type=MESH,
         )
 
-    def halo_start(*args):
-        for d in DIRS:
-            @pl.when(valid(d))
-            def _():
-                halo_copy(d, *args).start()
-
     def halo_wait(*args):
-        for d in DIRS:
-            @pl.when(valid(d))
-            def _():
-                halo_copy(opposite(d), *args).wait_recv()
+        halo_all(*args).wait_recv()
 
     def halo_sent(*args):
-        for d in DIRS:
-            @pl.when(valid(d))
-            def _():
-                halo_copy(d, *args).wait_send()
+        halo_all(*args).wait_send()
 
     def build(pad, stacked, reverse):
         pad3 = pad.reshape((T + 2) * (T + 2), ZS, C)
@@ -218,7 +205,7 @@
         stage(d, pad_i, send_a, OFFS[INDEX[d]] * 2)
         stage(d, pad_g, send_a, OFFS[INDEX[d]] * 2 + size)
     pl.semaphore_wait(barrier, count)
-    args_a = (send_a, recv_a, ha_send, ha_recv, 2)
+    args_a = (send_a, recv_a, ha_sems, 2)
     halo_start(*args_a)
 
     for g in range(2):
@@ -257,35 +244,24 @@
             total = term if total is None else total + term
         return total
 
-    pre_act = None
-    for a in range(3):
-        term = jnp.dot(slab(st_i, a), b1[a * K3:(a + 1) * K3, :], preferred_element_type=jnp.float32)
-        pre_act = term if pre_act is None else pre_act + term
-    back = conv_back(st_g, w2r)
-    sigma = 1.0 / (1.0 + jnp.exp(-pre_act))
-    hid_t[...] = (pre_act * sigma * keep).T.astype(jnp.bfloat16)
-    pre_grad = back * sigma * (1.0 + pre_act * (1.0 - sigma)) * keep
-    fill_own(pad_p, pre_grad)
-    pg_t[...] = pre_grad.T.astype(jnp.bfloat16)
-
-    names = dict(pair=n2, s1=3 * n2, s2=n2 - 1, zs=nz - 1, a2=n2 - 1, a1=3 * n2, a0=n1)
-    first_of = {}
-    total_sems = 0
-    for name, size in names.items():
-        first_of[name] = total_sems
-        total_sems += size
-    started = []
+    recv_first = dict(pair=0, s1=n2, s2=2 * n2, zs=2 * n2 + 1, a2=2 * n2 + 2, a1=3 * n2 + 1, a0=3 * n2 + n1)
+    send_index = {name: n for n, name in enumerate(recv_first)}
 
     def remote(src, dst, g, name, n, peer):
-        at = first_of[name] + n
         return pltpu.make_async_remote_copy(
-            src_ref=src, dst_ref=dst, send_sem=red_send.at[g, at], recv_sem=red_recv.at[g, at],
+            src_ref=src, dst_ref=dst,
+            send_sem=red_send.at[g, send_index[name]], recv_sem=red_recv.at[g, recv_first[name] + n],
             device_id=peer, device_id_type=MESH,
         )
 
+    def arrived(ref, g, name, n=0):
+        remote(ref, ref, g, name, n, partner).wait_recv()
+
+    def sent(ref, g, name):
+        remote(ref, ref, g, name, 0, partner).wait_send()
+
     def go(copy):
         copy.start()
-        started.append(copy)
 
     mine = pl.multiple_of(core * 64, 64)
     other = pl.multiple_of(64 - core * 64, 64)
@@ -294,7 +270,8 @@
     hop2 = (peer1, peer2)
 
     def chunk(g, i):
-        return (firsts[g][1] + 1 + i) % n2
+        own = firsts[g][1]
+        return own if i == n2 - 1 else i + (i >= own).astype(jnp.int32)
 
     def pair_copy(g, j):
         return remote(grads.at[g, j, pl.ds(other, 64)], r0.at[g, j], g, "pair", j, partner)
@@ -304,24 +281,25 @@
         return grads[g, j, pl.ds(mine + here, r1), :] + r0[g, j, pl.ds(here, r1), :]
 
     def s1_copy(g, i, k):
-        return remote(s1_send.at[g, i, k - 1], s1_recv.at[g, i, k - 1], g, "s1", 3 * i + k - 1, hop1[g](k))
-
-    def s2_copy(g, k):
-        return remote(s2_send.at[g, k - 1], s2_recv.at[g, k - 1], g, "s2", k - 1, hop2[g](k))
-
-    def z_copy(g, k, wait):
-        ref = z_all.at[g, (cz + (nz - k)) % nz if wait else cz]
-        return remote(ref, ref, g, "zs", k - 1, peerz(k))
+        return remote(s1_send.at[g, i, k - 1], s1_recv.at[g, i, k - 1], g, "s1", i, hop1[g](k))
+
+    def s2_copy(g, i):
+        k = (chunk(g, i) - firsts[g][1] + n2) % n2
+        return remote(s2_send.at[g, i], s2_recv.at[g, k - 1], g, "s2", 0, hop2[g](k))
+
+    def z_copy(g, k):
+        ref = z_all.at[g, cz]
+        return remote(ref, ref, g, "zs", 0, peerz(k))
 
     def a2_copy(g, k, wait):
         b, j = firsts[g]
         ref = ag.at[g, core, b, (j + (n2 - k)) % n2 if wait else j]
         return remote(ref, ref, g, "a2", k - 1, hop2[g](k))
 
-    def a1_copy(g, m, k, wait):
+    def a1_copy(g, m, k):
         b, j = firsts[g]
-        ref = ag.at[g, core, (b + (n1 - k)) % n1 if wait else b, (j + (n2 - m)) % n2]
-        return remote(ref, ref, g, "a1", 3 * m + k - 1, hop1[g](k))
+        ref = ag.at[g, core, b, (j + (n2 - m)) % n2]
+        return remote(ref, ref, g, "a1", k - 1, hop1[g](k))
 
     def a0_copy(g, n, wait):
         ref = ag.at[g, 1 - core if wait else core, (firsts[g][1 if wait else 0] + (n1 - n)) % n1]
@@ -352,12 +330,12 @@
     def scatter2(g):
         for i in range(n2):
             total = chip(g, chunk(g, i), firsts[g][0])
+            arrived(s1_recv.at[g, i], g, "s1", i)
             for k in range(1, n1):
-                s1_copy(g, i, k).wait_recv()
                 total = total + s1_recv[g, i, k - 1].astype(jnp.float32)
             if i < n2 - 1:
                 s2_send[g, i] = total
-                go(s2_copy(g, i + 1))
+                go(s2_copy(g, i))
             else:
                 s1_own[g] = total
 
@@ -365,16 +343,15 @@
 
     def scatter3(g):
         total = s1_own[g]
+        arrived(s2_recv.at[g], g, "s2")
         for k in range(1, n2):
-            s2_copy(g, k).wait_recv()
             total = total + s2_recv[g, k - 1]
         z_all[g, cz] = total.astype(jnp.bfloat16)
         for k in z_order:
-            go(z_copy(g, k, False))
+            go(z_copy(g, k))
 
     def gather2(g):
-        for k in reversed(z_order):
-            z_copy(g, k, True).wait_recv()
+        arrived(z_all.at[g, pl.ds(0, nz - 1)], g, "zs")
         total = z_all[g, 0].astype(jnp.float32)
         for z in range(1, nz):
             total = total + z_all[g, z].astype(jnp.float32)
@@ -383,105 +360,126 @@
         for k in far_first:
             go(a2_copy(g, k, False))
         for k in far_first:
-            go(a1_copy(g, 0, k, False))
+            go(a1_copy(g, 0, k))
 
     def gather1(g):
         for m in (1, 3, 2):
             a2_copy(g, m, True).wait_recv()
             for k in far_first:
-                go(a1_copy(g, m, k, False))
+                go(a1_copy(g, m, k))
         go(a0_copy(g, 0, False))
+        put(g, core, firsts[g][0])
 
     def gather0(g):
         for k in (1, 3, 2):
-            for m in (0, 1, 3, 2):
-                a1_copy(g, m, k, True).wait_recv()
+            block = (firsts[g][0] + (n1 - k)) % n1
+            arrived(ag.at[g, core, block], g, "a1", k - 1)
             go(a0_copy(g, k, False))
+            put(g, core, block)
+
+    def put(g, half, block):
+        copy = pltpu.make_async_copy(ag.at[g, half, block], ag_out.at[g, half, block], out_sem.at[0])
+        copy.start()
 
     def finish(g):
         for n in (0, 1, 3, 2):
             a0_copy(g, n, True).wait_recv()
-        done = pltpu.make_async_copy(ag.at[g], ag_out.at[g], load_sem.at[4 + g])
-        done.start()
-        return done
-
+            put(g, 1 - core, (firsts[g][1] + (n1 - n)) % n1)
+
+    pre_act = None
+    for a in range(3):
+        term = jnp.dot(slab(st_i, a), b1[a * K3:(a + 1) * K3, :], preferred_element_type=jnp.float32)
+        pre_act = term if pre_act is None else pre_act + term
+    sigma = 1.0 / (1.0 + jnp.exp(-pre_act))
+    hid_t[...] = (pre_act * sigma * keep).T.astype(jnp.bfloat16)
+    corr(0, hid_t, lambda a: slab(st_g, 2 - a))
+    back = conv_back(st_g, w2r)
+    pre_grad = back * sigma * (1.0 + pre_act * (1.0 - sigma)) * keep
+    fill_own(pad_p, pre_grad)
+    pg_t[...] = pre_grad.T.astype(jnp.bfloat16)
+    scatter1(0)
     corr(1, pg_t, lambda a: slab(st_i, a))
-    corr(0, hid_t, lambda a: slab(st_g, 2 - a))
     scatter1(1)
-    scatter1(0)
     for d in DIRS:
         stage(d, pad_p, send_b, OFFS[INDEX[d]])
-    args_b = (send_b, recv_b, hb_send, hb_recv, 1)
+    args_b = (send_b, recv_b, hb_sems, 1)
     halo_start(*args_b)
+    scatter2(0)
     scatter2(1)
-    scatter2(0)
+    scatter3(0)
     halo_wait(*args_b)
     for d in DIRS:
         fill_halo(d, pad_p, recv_b, OFFS[INDEX[d]])
     build(pad_p, st_p, True)
     scatter3(1)
-    scatter3(0)
     result = conv_back(st_p, w1r)
-    fg_ref[...] = ((cot[...].astype(jnp.float32) * keep + result) * keep).astype(jnp.bfloat16)
+    fg[...] = ((cot[...].astype(jnp.float32) * keep + result) * keep).astype(jnp.bfloat16)
+    fg_copy = pltpu.make_async_copy(fg, fg_out, load_sem.at[0])
+    fg_copy.start()
+    gather2(0)
     gather2(1)
-    gather2(0)
+    gather1(0)
     gather1(1)
-    gather1(0)
+    gather0(0)
     gather0(1)
-    gather0(0)
-    done1 = finish(1)
-    done0 = finish(0)
+    finish(0)
+    finish(1)
 
     halo_sent(*args_a)
     halo_sent(*args_b)
-    for copy in started:
-        copy.wait_send()
-    done1.wait()
-    done0.wait()
-
-
-def unpack_kernel(plan, ag_hbm, fg_hbm, g1_hbm, g2_hbm, fg_out, ag, fg, g1, g2, sems):
+    for g in range(2):
+        sent(r0.at[g], g, "pair")
+        sent(s1_send.at[g], g, "s1")
+        sent(s2_send.at[g], g, "s2")
+        sent(z_all.at[g, pl.ds(0, nz - 1)], g, "zs")
+        sent(s1_send.at[g, 0], g, "a2")
+        sent(s1_send.at[g], g, "a1")
+        sent(ag.at[g, core], g, "a0")
+    fg_copy.wait()
+    pltpu.make_async_copy(ag, ag_out, out_sem.at[0]).wait()
+
+
+def unpack_kernel(plan, ag_hbm, fg_hbm, g1_hbm, g2_hbm, fg_out, ag, fg, g1, g2, sems, store_sem):
     n1, r1, t2 = plan.nx, plan.r1, plan.t2
     rows = r1 * TAPS
-    loads = [
-        pltpu.make_async_copy(src, dst, sems.at[n])
-        for n, (src, dst) in enumerate(((ag_hbm.at[0], ag.at[0]), (ag_hbm.at[1], ag.at[1]), (fg_hbm, fg)))
-    ]
-    for copy in loads:
-        copy.start()
-    stores = []
-
-    def put(src, dst):
-        copy = pltpu.make_async_copy(src, dst, sems.at[3 + len(stores)])
-        copy.start()
-        stores.append(copy)
-
-    loads[0].wait()
-    for half in range(2):
-        for block in range(n1):
-            first = (half * n1 + block) * rows
-            for tap in range(TAPS):
-                lanes = pl.ds(tap % t2 * C, C)
-                g2[pl.ds(first + tap, r1, stride=TAPS), :] = (
-                    ag[0, half, block, tap // t2, :, lanes].astype(jnp.float32)
-                )
-            put(g2.at[pl.ds(first, rows)], g2_hbm.at[pl.ds(first, rows)])
-    loads[2].wait()
-    put(fg, fg_out)
-    loads[1].wait()
+    blocks = [(half, block) for half in range(2) for block in range(n1)]
+
+    def load(g, half, block):
+        return pltpu.make_async_copy(ag_hbm.at[g, half, block], ag.at[g, half, block], sems.at[g, half, block])
+
+    for g in range(2):
+        for half, block in blocks:
+            load(g, half, block).start()
+    load_fg = pltpu.make_async_copy(fg_hbm, fg, store_sem.at[2])
+    load_fg.start()
+    for half, block in blocks:
+        load(0, half, block).wait()
+        first = (half * n1 + block) * rows
+        for tap in range(TAPS):
+            g2[pl.ds(first + tap, r1, stride=TAPS), :] = (
+                ag[0, half, block, tap // t2, :, pl.ds(tap % t2 * C, C)].astype(jnp.float32)
+            )
+        pltpu.make_async_copy(g2.at[pl.ds(first, rows)], g2_hbm.at[pl.ds(first, rows)], store_sem.at[0]).start()
+    for half, block in blocks:
+        load(1, half, block).wait()
     for tap in range(TAPS):
-        block = ag[1, :, :, tap // t2, :, pl.ds(tap % t2 * C, C)].reshape(C, C)
-        g1[pl.ds(tap, C, stride=TAPS), :] = block.astype(jnp.float32).T
-    put(g1, g1_hbm)
-    for copy in stores:
-        copy.wait()
+        square = ag[1, :, :, tap // t2, :, pl.ds(tap % t2 * C, C)].reshape(C, C)
+        g1[pl.ds(tap, C, stride=TAPS), :] = square.astype(jnp.float32).T
+    for n in range(2 * n1):
+        part = pl.ds(n * rows, rows)
+        pltpu.make_async_copy(g1.at[part], g1_hbm.at[part], store_sem.at[1]).start()
+    load_fg.wait()
+    store_fg = pltpu.make_async_copy(fg, fg_out, store_sem.at[2])
+    store_fg.start()
+    pltpu.make_async_copy(g2, g2_hbm, store_sem.at[0]).wait()
+    pltpu.make_async_copy(g1, g1_hbm, store_sem.at[1]).wait()
+    store_fg.wait()
 
 
 def on_device(plan, features, tile_mask, w_first, w_second, cotangent):
     n1, n2, nz, r1, t2 = plan.nx, plan.ny, plan.nz, plan.r1, plan.t2
     f32, bf16 = jnp.float32, jnp.bfloat16
     rows = TAPS * C
-    copies = 7 * n2 + n1 + 2 * (n2 - 1) + nz - 1
     gathered = (2, 2, n1, n2, r1, t2 * C)
     s1_buf = pltpu.VMEM((2, n2, n1 - 1, r1, t2 * C), bf16)
     s2_buf = pltpu.VMEM((2, n2 - 1, r1, t2 * C), f32)
@@ -491,7 +489,6 @@
     halo_b = pltpu.VMEM((TILES, 8, C), bf16)
     dma = pltpu.SemaphoreType.DMA
     any_spec = pl.BlockSpec(memory_space=pl.ANY)
-    vmem_spec = pl.BlockSpec(memory_space=pltpu.VMEM)
     scratch = [
         pltpu.VMEM((512, C), bf16), pltpu.VMEM((512, C), bf16),
         pltpu.VMEM((rows, C), bf16), pltpu.VMEM((rows, C), bf16), pltpu.VMEM((rows, C), f32),
@@ -502,15 +499,14 @@
         pltpu.VMEM((2, n2, C, t2 * C), f32), pltpu.VMEM((2, n2, 64, t2 * C), f32),
         s1_buf, s1_buf, pltpu.VMEM((2, r1, t2 * C), f32), s2_buf, s2_buf,
         pltpu.VMEM((2, nz, r1, t2 * C), bf16),
-        pltpu.VMEM(gathered, bf16),
-        dma((6,)), dma((26,)), dma((26,)), dma((26,)), dma((26,)),
-        dma((2, copies)), dma((2, copies)),
+        pltpu.VMEM(gathered, bf16), pltpu.VMEM((512, C), bf16),
+        dma((4,)), dma((1,)), dma((2,)), dma((2,)), dma((2, 7)), dma((2, 3 * n2 + 2 * n1)),
     ]
     partial_fg, partial_ag = pl.pallas_call(
         functools.partial(kernel, plan),
         out_shape=(jax.ShapeDtypeStruct((512, C), bf16), jax.ShapeDtypeStruct(gathered, bf16)),
         in_specs=[pl.BlockSpec(memory_space=pltpu.SMEM)] + [any_spec] * 4,
-        out_specs=(vmem_spec, any_spec),
+        out_specs=(any_spec,) * 2,
         scratch_shapes=scratch,
         compiler_params=pltpu.CompilerParams(collective_id=0, has_side_effects=True),
         name="block_backward",
@@ -526,7 +522,7 @@
         out_specs=(any_spec,) * 3,
         scratch_shapes=[
             pltpu.VMEM(gathered, bf16), pltpu.VMEM((512, C), bf16),
-            pltpu.VMEM((rows, C), f32), pltpu.VMEM((rows, C), f32), dma((3 + 2 * n1 + 2,)),
+            pltpu.VMEM((rows, C), f32), pltpu.VMEM((rows, C), f32), dma((2, 2, n1)), dma((3,)),
         ],
         name="unpack",
     )(partial_ag, partial_fg)

time: 59.7 us -> 56.9 us (0.953)
  Pallas kernels: 58.3 us -> 55.4 us
    pallas_call x1, Pallas kernels: 55.2 us -> 52.2 us  [on_device(): pl.pallas_call(functools.partial(kernel, plan), out_shape=(jax.ShapeDtype...]
where the time goes in v3:
time: 56.9 us; the launch traced here: 56.7 us
  Pallas kernels  55.4 us (97%)
  between operations  1.28 us (2%)
    pallas_call x1, Pallas kernels, on_device(): pl.pallas_call(functools.partial(kernel, plan), out_shape=(jax.ShapeDtype...  52.2 us
    pallas_call x1, Pallas kernels, on_device(): pl.pallas_call(functools.partial(unpack_kernel, plan), out_shape=(jax.Sha...  3.24 us

profile of v3, /device:TPU:1, one launch (start us, length us, event | category | flops | bytes accessed | tf_op | source)
XLA Modules:
  0.0 56.7 jit_solution(14573319809374661951)
XLA Ops:
  1.3 52.2 %block_backward.1 = (bf16[512,128]{1,0:T(8,128)(2,1)}, bf16[2,2,4,4,16,896]{5,4,3,2,1,0:T(8,128)(2,1)}) custom-call(s32[1,1]{1,0:T(1,128)S(6)} %copy.8.mask_ref, bf16[512,128]{1,0:T(8,128)(2,1)} %bitcast.3, bf16[512,128]{1,0:T(8,128)(2,1)} %bitcast.4, bf16[3456,128]{1,0:T(8,128)(2,1)} %w1_hbm.1, bf16[3456,128]{1,0:T(8,128)(2,1)} %w2_hbm.1), custom_call_target="tpu_custom_call" | custom-call | tf_op jit(solution)/shard_map/block_backward/pallas_call | solution.py:505
  53.5 3.2 %unpack.1 = (f32[3456,128]{1,0:T(8,128)}, f32[3456,128]{1,0:T(8,128)}, bf16[512,128]{1,0:T(8,128)(2,1)}) custom-call(bf16[2,2,4,4,16,896]{5,4,3,2,1,0:T(8,128)(2,1)} %get-tuple-element.8.ag_hbm, bf16[512,128]{1,0:T(8,128)(2,1)} %get-tuple-element.9.fg_hbm), custom_call_target="tpu_custom_call" | custom-call | tf_op jit(solution)/shard_map/unpack/pallas_call | solution.py:514

commit v4 on v3

--- a/solution.py
+++ b/solution.py
@@ -68,13 +68,13 @@
 def kernel(
     plan,
     mask_ref, feat_hbm, cot_hbm, w1_hbm, w2_hbm,
-    fg_out, ag_out,
+    fg, ag,
     feat, cot, w1, w2, wf, w1r, w2r, b1,
     pad_i, pad_g, pad_p, st_i, st_g, st_p,
     send_a, recv_a, send_b, recv_b,
     pg_t, hid_t,
-    grads, r0, s1_send, s1_recv, s1_own, s2_send, s2_recv, z_all, ag, fg,
-    load_sem, out_sem, ha_sems, hb_sems, red_send, red_recv,
+    grads, r0, s1_send, s1_recv, s1_own, s2_send, s2_recv, z_all,
+    load_sem, ha_sems, hb_sems, red_send, red_recv,
 ):
     nz, nx, ny = plan.nz, plan.nx, plan.ny
     n1, n2, r1, t2 = nx, ny, plan.r1, plan.t2
@@ -368,23 +368,16 @@
             for k in far_first:
                 go(a1_copy(g, m, k))
         go(a0_copy(g, 0, False))
-        put(g, core, firsts[g][0])
 
     def gather0(g):
         for k in (1, 3, 2):
             block = (firsts[g][0] + (n1 - k)) % n1
             arrived(ag.at[g, core, block], g, "a1", k - 1)
             go(a0_copy(g, k, False))
-            put(g, core, block)
-
-    def put(g, half, block):
-        copy = pltpu.make_async_copy(ag.at[g, half, block], ag_out.at[g, half, block], out_sem.at[0])
-        copy.start()
 
     def finish(g):
         for n in (0, 1, 3, 2):
             a0_copy(g, n, True).wait_recv()
-            put(g, 1 - core, (firsts[g][1] + (n1 - n)) % n1)
 
     pre_act = None
     for a in range(3):
@@ -399,9 +392,9 @@
     pg_t[...] = pre_grad.T.astype(jnp.bfloat16)
     scatter1(0)
     corr(1, pg_t, lambda a: slab(st_i, a))
-    scatter1(1)
     for d in DIRS:
         stage(d, pad_p, send_b, OFFS[INDEX[d]])
+    scatter1(1)
     args_b = (send_b, recv_b, hb_sems, 1)
     halo_start(*args_b)
     scatter2(0)
@@ -414,8 +407,6 @@
     scatter3(1)
     result = conv_back(st_p, w1r)
     fg[...] = ((cot[...].astype(jnp.float32) * keep + result) * keep).astype(jnp.bfloat16)
-    fg_copy = pltpu.make_async_copy(fg, fg_out, load_sem.at[0])
-    fg_copy.start()
     gather2(0)
     gather2(1)
     gather1(0)
@@ -435,42 +426,28 @@
         sent(s1_send.at[g, 0], g, "a2")
         sent(s1_send.at[g], g, "a1")
         sent(ag.at[g, core], g, "a0")
-    fg_copy.wait()
-    pltpu.make_async_copy(ag, ag_out, out_sem.at[0]).wait()
-
-
-def unpack_kernel(plan, ag_hbm, fg_hbm, g1_hbm, g2_hbm, fg_out, ag, fg, g1, g2, sems, store_sem):
+
+
+def unpack_kernel(plan, ag, fg, g1_hbm, g2_hbm, fg_out, g1, g2, store_sem):
     n1, r1, t2 = plan.nx, plan.r1, plan.t2
     rows = r1 * TAPS
     blocks = [(half, block) for half in range(2) for block in range(n1)]
 
-    def load(g, half, block):
-        return pltpu.make_async_copy(ag_hbm.at[g, half, block], ag.at[g, half, block], sems.at[g, half, block])
-
-    for g in range(2):
-        for half, block in blocks:
-            load(g, half, block).start()
-    load_fg = pltpu.make_async_copy(fg_hbm, fg, store_sem.at[2])
-    load_fg.start()
+    store_fg = pltpu.make_async_copy(fg, fg_out, store_sem.at[2])
+    store_fg.start()
     for half, block in blocks:
-        load(0, half, block).wait()
         first = (half * n1 + block) * rows
         for tap in range(TAPS):
             g2[pl.ds(first + tap, r1, stride=TAPS), :] = (
                 ag[0, half, block, tap // t2, :, pl.ds(tap % t2 * C, C)].astype(jnp.float32)
             )
         pltpu.make_async_copy(g2.at[pl.ds(first, rows)], g2_hbm.at[pl.ds(first, rows)], store_sem.at[0]).start()
-    for half, block in blocks:
-        load(1, half, block).wait()
     for tap in range(TAPS):
         square = ag[1, :, :, tap // t2, :, pl.ds(tap % t2 * C, C)].reshape(C, C)
         g1[pl.ds(tap, C, stride=TAPS), :] = square.astype(jnp.float32).T
     for n in range(2 * n1):
         part = pl.ds(n * rows, rows)
         pltpu.make_async_copy(g1.at[part], g1_hbm.at[part], store_sem.at[1]).start()
-    load_fg.wait()
-    store_fg = pltpu.make_async_copy(fg, fg_out, store_sem.at[2])
-    store_fg.start()
     pltpu.make_async_copy(g2, g2_hbm, store_sem.at[0]).wait()
     pltpu.make_async_copy(g1, g1_hbm, store_sem.at[1]).wait()
     store_fg.wait()
@@ -488,6 +465,7 @@
     halo_a = pltpu.VMEM((2 * TILES, 8, C), bf16)
     halo_b = pltpu.VMEM((TILES, 8, C), bf16)
     dma = pltpu.SemaphoreType.DMA
+    vmem_spec = pl.BlockSpec(memory_space=pltpu.VMEM)
     any_spec = pl.BlockSpec(memory_space=pl.ANY)
     scratch = [
         pltpu.VMEM((512, C), bf16), pltpu.VMEM((512, C), bf16),
@@ -499,16 +477,17 @@
         pltpu.VMEM((2, n2, C, t2 * C), f32), pltpu.VMEM((2, n2, 64, t2 * C), f32),
         s1_buf, s1_buf, pltpu.VMEM((2, r1, t2 * C), f32), s2_buf, s2_buf,
         pltpu.VMEM((2, nz, r1, t2 * C), bf16),
-        pltpu.VMEM(gathered, bf16), pltpu.VMEM((512, C), bf16),
-        dma((4,)), dma((1,)), dma((2,)), dma((2,)), dma((2, 7)), dma((2, 3 * n2 + 2 * n1)),
+        dma((4,)), dma((2,)), dma((2,)), dma((2, 7)), dma((2, 3 * n2 + 2 * n1)),
     ]
     partial_fg, partial_ag = pl.pallas_call(
         functools.partial(kernel, plan),
-        out_shape=(jax.ShapeDtypeStruct((512, C), bf16), jax.ShapeDtypeStruct(gathered, bf16)),
+        out_shape=(pltpu.VMEM((512, C), bf16), pltpu.VMEM(gathered, bf16)),
         in_specs=[pl.BlockSpec(memory_space=pltpu.SMEM)] + [any_spec] * 4,
-        out_specs=(any_spec,) * 2,
+        out_specs=(vmem_spec,) * 2,
         scratch_shapes=scratch,
-        compiler_params=pltpu.CompilerParams(collective_id=0, has_side_effects=True),
+        compiler_params=pltpu.CompilerParams(
+            collective_id=0, has_side_effects=True, vmem_limit_bytes=56 * 1024 * 1024
+        ),
         name="block_backward",
     )(tile_mask, features[0], cotangent[0], w_first, w_second)
     grad_first, grad_second, feature_grad = pl.pallas_call(
@@ -518,12 +497,12 @@
             jax.ShapeDtypeStruct((rows, C), f32),
             jax.ShapeDtypeStruct((512, C), bf16),
         ),
-        in_specs=[any_spec] * 2,
+        in_specs=[vmem_spec] * 2,
         out_specs=(any_spec,) * 3,
         scratch_shapes=[
-            pltpu.VMEM(gathered, bf16), pltpu.VMEM((512, C), bf16),
-            pltpu.VMEM((rows, C), f32), pltpu.VMEM((rows, C), f32), dma((2, 2, n1)), dma((3,)),
+            pltpu.VMEM((rows, C), f32), pltpu.VMEM((rows, C), f32), dma((3,)),
         ],
+        compiler_params=pltpu.CompilerParams(vmem_limit_bytes=16 * 1024 * 1024),
         name="unpack",
     )(partial_ag, partial_fg)
     return grad_first, grad_second, feature_grad[None]

time: 56.9 us -> 55 us (0.967)
  Pallas kernels: 55.4 us -> 53.6 us
    pallas_call x1, Pallas kernels: 3.24 us -> 2.05 us  [on_device(): pl.pallas_call(functools.partial(unpack_kernel, plan), out_shape=(jax.Sha...]
    pallas_call x1, Pallas kernels: 52.2 us -> 51.5 us  [on_device(): pl.pallas_call(functools.partial(kernel, plan), out_shape=(pltpu.VMEM((51...]
where the time goes in v4:
time: 55 us; the launch traced here: 54.9 us
  Pallas kernels  53.6 us (97%)
  between operations  1.28 us (2%)
    pallas_call x1, Pallas kernels, on_device(): pl.pallas_call(functools.partial(kernel, plan), out_shape=(pltpu.VMEM((51...  51.5 us
    pallas_call x1, Pallas kernels, on_device(): pl.pallas_call(functools.partial(unpack_kernel, plan), out_shape=(jax.Sha...  2.05 us

profile of v4, /device:TPU:1, one launch (start us, length us, event | category | flops | bytes accessed | tf_op | source)
XLA Modules:
  0.0 54.9 jit_solution(13172223458394475110)
XLA Ops:
  1.3 51.5 %block_backward.1 = (bf16[512,128]{1,0:T(8,128)(2,1)S(1)}, bf16[2,2,4,4,16,896]{5,4,3,2,1,0:T(8,128)(2,1)S(1)}) custom-call(s32[1,1]{1,0:T(1,128)S(6)} %copy.8.mask_ref, bf16[512,128]{1,0:T(8,128)(2,1)} %bitcast.3, bf16[512,128]{1,0:T(8,128)(2,1)} %bitcast.4, bf16[3456,128]{1,0:T(8,128)(2,1)} %w1_hbm.1, bf16[3456,128]{1,0:T(8,128)(2,1)} %w2_hbm.1), custom_call_target="tpu_custom_call" | custom-call | tf_op jit(solution)/shard_map/block_backward/pallas_call | solution.py:482
  52.8 2.1 %unpack.1 = (f32[3456,128]{1,0:T(8,128)}, f32[3456,128]{1,0:T(8,128)}, bf16[512,128]{1,0:T(8,128)(2,1)}) custom-call(bf16[2,2,4,4,16,896]{5,4,3,2,1,0:T(8,128)(2,1)S(1)} %get-tuple-element.8.ag, bf16[512,128]{1,0:T(8,128)(2,1)S(1)} %get-tuple-element.9.fg), custom_call_target="tpu_custom_call" | custom-call | tf_op jit(solution)/shard_map/unpack/pallas_call | solution.py:493

commit v5 on v4

--- a/solution.py
+++ b/solution.py
@@ -317,7 +317,7 @@
                 go(pair_copy(g, sent))
                 sent += 1
 
-    far_first = (2, 1, 3)
+    far_first = (3, 2, 1)
 
     def scatter1(g):
         for i in range(n2):
@@ -334,7 +334,7 @@
             for k in range(1, n1):
                 total = total + s1_recv[g, i, k - 1].astype(jnp.float32)
             if i < n2 - 1:
-                s2_send[g, i] = total
+                s2_send[g, i] = total.astype(jnp.bfloat16)
                 go(s2_copy(g, i))
             else:
                 s1_own[g] = total
@@ -345,7 +345,7 @@
         total = s1_own[g]
         arrived(s2_recv.at[g], g, "s2")
         for k in range(1, n2):
-            total = total + s2_recv[g, k - 1]
+            total = total + s2_recv[g, k - 1].astype(jnp.float32)
         z_all[g, cz] = total.astype(jnp.bfloat16)
         for k in z_order:
             go(z_copy(g, k))
@@ -459,7 +459,7 @@
     rows = TAPS * C
     gathered = (2, 2, n1, n2, r1, t2 * C)
     s1_buf = pltpu.VMEM((2, n2, n1 - 1, r1, t2 * C), bf16)
-    s2_buf = pltpu.VMEM((2, n2 - 1, r1, t2 * C), f32)
+    s2_buf = pltpu.VMEM((2, n2 - 1, r1, t2 * C), bf16)
     pad = pltpu.VMEM(((T + 2) * (T + 2) * ZS, C), f32)
     stacked = pltpu.VMEM((T + 2, 64, K3), bf16)
     halo_a = pltpu.VMEM((2 * TILES, 8, C), bf16)

time: 55 us -> 54.5 us (level)
  no operation moved by 1% of the time
where the time goes in v5:
time: 54.5 us; the launch traced here: 54.3 us
  Pallas kernels  53.1 us (97%)
  between operations  1.28 us (2%)
    pallas_call x1, Pallas kernels, on_device(): pl.pallas_call(functools.partial(kernel, plan), out_shape=(pltpu.VMEM((51...  51 us
    pallas_call x1, Pallas kernels, on_device(): pl.pallas_call(functools.partial(unpack_kernel, plan), out_shape=(jax.Sha...  2.05 us

profile of v5, /device:TPU:1, one launch (start us, length us, event | category | flops | bytes accessed | tf_op | source)
XLA Modules:
  0.0 54.3 jit_solution(13110008349278413475)
XLA Ops:
  1.3 51.0 %block_backward.1 = (bf16[512,128]{1,0:T(8,128)(2,1)S(1)}, bf16[2,2,4,4,16,896]{5,4,3,2,1,0:T(8,128)(2,1)S(1)}) custom-call(s32[1,1]{1,0:T(1,128)S(6)} %copy.8.mask_ref, bf16[512,128]{1,0:T(8,128)(2,1)} %bitcast.3, bf16[512,128]{1,0:T(8,128)(2,1)} %bitcast.4, bf16[3456,128]{1,0:T(8,128)(2,1)} %w1_hbm.1, bf16[3456,128]{1,0:T(8,128)(2,1)} %w2_hbm.1), custom_call_target="tpu_custom_call" | custom-call | tf_op jit(solution)/shard_map/block_backward/pallas_call | solution.py:482
  52.3 2.1 %unpack.1 = (f32[3456,128]{1,0:T(8,128)}, f32[3456,128]{1,0:T(8,128)}, bf16[512,128]{1,0:T(8,128)(2,1)}) custom-call(bf16[2,2,4,4,16,896]{5,4,3,2,1,0:T(8,128)(2,1)S(1)} %get-tuple-element.8.ag, bf16[512,128]{1,0:T(8,128)(2,1)S(1)} %get-tuple-element.9.fg), custom_call_target="tpu_custom_call" | custom-call | tf_op jit(solution)/shard_map/unpack/pallas_call | solution.py:493

commit v6 on v5

--- a/solution.py
+++ b/solution.py
@@ -363,20 +363,20 @@
             go(a1_copy(g, 0, k))
 
     def gather1(g):
-        for m in (1, 3, 2):
+        for m in (3, 1, 2):
             a2_copy(g, m, True).wait_recv()
             for k in far_first:
                 go(a1_copy(g, m, k))
         go(a0_copy(g, 0, False))
 
     def gather0(g):
-        for k in (1, 3, 2):
+        for k in (3, 1, 2):
             block = (firsts[g][0] + (n1 - k)) % n1
             arrived(ag.at[g, core, block], g, "a1", k - 1)
             go(a0_copy(g, k, False))
 
     def finish(g):
-        for n in (0, 1, 3, 2):
+        for n in (0, 3, 1, 2):
             a0_copy(g, n, True).wait_recv()
 
     pre_act = None

time: 54.5 us -> 53.5 us (0.982)
  Pallas kernels: 53.1 us -> 52.1 us
    pallas_call x1, Pallas kernels: 51 us -> 50.1 us  [on_device(): pl.pallas_call(functools.partial(kernel, plan), out_shape=(pltpu.VMEM((51...]
where the time goes in v6:
time: 53.5 us; the launch traced here: 53.4 us
  Pallas kernels  52.1 us (97%)
  between operations  1.28 us (2%)
    pallas_call x1, Pallas kernels, on_device(): pl.pallas_call(functools.partial(kernel, plan), out_shape=(pltpu.VMEM((51...  50.1 us
    pallas_call x1, Pallas kernels, on_device(): pl.pallas_call(functools.partial(unpack_kernel, plan), out_shape=(jax.Sha...  2.05 us

profile of v6, /device:TPU:1, one launch (start us, length us, event | category | flops | bytes accessed | tf_op | source)
XLA Modules:
  0.0 53.4 jit_solution(17484259661488387995)
XLA Ops:
  1.3 50.1 %block_backward.1 = (bf16[512,128]{1,0:T(8,128)(2,1)S(1)}, bf16[2,2,4,4,16,896]{5,4,3,2,1,0:T(8,128)(2,1)S(1)}) custom-call(s32[1,1]{1,0:T(1,128)S(6)} %copy.8.mask_ref, bf16[512,128]{1,0:T(8,128)(2,1)} %bitcast.3, bf16[512,128]{1,0:T(8,128)(2,1)} %bitcast.4, bf16[3456,128]{1,0:T(8,128)(2,1)} %w1_hbm.1, bf16[3456,128]{1,0:T(8,128)(2,1)} %w2_hbm.1), custom_call_target="tpu_custom_call" | custom-call | tf_op jit(solution)/shard_map/block_backward/pallas_call | solution.py:482
  51.4 2.1 %unpack.1 = (f32[3456,128]{1,0:T(8,128)}, f32[3456,128]{1,0:T(8,128)}, bf16[512,128]{1,0:T(8,128)(2,1)}) custom-call(bf16[2,2,4,4,16,896]{5,4,3,2,1,0:T(8,128)(2,1)S(1)} %get-tuple-element.8.ag, bf16[512,128]{1,0:T(8,128)(2,1)S(1)} %get-tuple-element.9.fg), custom_call_target="tpu_custom_call" | custom-call | tf_op jit(solution)/shard_map/unpack/pallas_call | solution.py:493
